TPU v7x, 32 devices: a whole 2x2x4 slice. The times are simulated.
32 devices in a mesh: pipe: 4 (over z), expert: 8 (over y, x, core).
Axes of the slice: x: 2, y: 2, z: 4, core: 2. Of those that a mesh axis runs over, the one named last changes fastest.
Arguments:
- fwd_state: bfloat16 [4, 192, 3584], P('pipe', 'expert'), may hold values from -6 to 6
- bwd_state: bfloat16 [4, 192, 3584], P('pipe', 'expert'), may hold values from -6 to 6
- saved_input: bfloat16 [4, 2, 192, 3584], P('pipe', None, 'expert'), may hold values from -6 to 6
- fwd_route: int32 [4, 2, 192, 1], P('pipe', None, 'expert'), may hold values from 0 to 3; in each aligned block of 24 rows (0 to 23, 24 to 47, ..., all dimensions but the last counted through in order) at most 7 rows name the same one
- bwd_route: int32 [4, 2, 192, 1], P('pipe', None, 'expert'), may hold values from 0 to 3; in each aligned block of 24 rows (0 to 23, 24 to 47, ..., all dimensions but the last counted through in order) at most 7 rows name the same one
- fwd_gate: float32 [4, 2, 192], P('pipe', None, 'expert'), may hold values from 0.3 to 1
- bwd_gate: float32 [4, 2, 192], P('pipe', None, 'expert'), may hold values from 0.3 to 1
- w_gate: bfloat16 [4, 3584, 1024], P('pipe', None, 'expert'), may hold values from -0.09375 to 0.09375
- w_up: bfloat16 [4, 3584, 1024], P('pipe', None, 'expert'), may hold values from -0.09375 to 0.09375
- w_down: bfloat16 [4, 1024, 3584], P('pipe', 'expert'), may hold values from -0.375 to 0.375
- norm_gain: float32 [4, 3584], P('pipe'), may hold values from 0.5 to 1.5
Outputs:
- fwd_out: bfloat16 [4, 192, 3584], P('pipe', 'expert')
- bwd_out: bfloat16 [4, 192, 3584], P('pipe', 'expert')
Inputs may be any that keep to these rules, and one draw needn't show every extreme that they name: `fwd_route`: in the rows of one device at one rank and step, no expert is named more than 7 times, and one is named exactly 7 times. `bwd_route`: as for fwd_route.
All inputs are finite; a program needn't handle non-finite values.
Results may differ from a plain program's by a relative error of at most 0.0068.
Values may be sent and summed in bfloat16 or wider, within the bound.
No kernel may reach another device: no remote copies, remote signals or barrier semaphores. Data moves between devices by JAX's collectives and lax.ppermute only.
A program may use at most 64 MiB of HBM per device.

v0:
```python
import jax
import jax.numpy as jnp
from jax import lax
from jax.sharding import PartitionSpec as P

EXPERTS = 4
CAP = 7


EPS = 1e-06


def passed_along(array, axis, by):
    size = lax.axis_size(axis)
    pairs = [(i, i + by) for i in range(size) if 0 <= i + by < size]
    return lax.ppermute(array, axis, pairs)


def norm_rows(rows, gain):
    raw = rows.astype(jnp.float32)
    scale = lax.rsqrt(jnp.mean(raw * raw, axis=-1, keepdims=True) + EPS)
    return (raw, scale, (raw * scale * gain).astype(jnp.bfloat16))


def slot_index(route):
    hits = (route[:, None] == jnp.arange(EXPERTS, dtype=jnp.int32)[None, :]).astype(jnp.int32)
    before = jnp.cumsum(hits, axis=0) - hits
    return route * CAP + jnp.sum(before * hits, axis=1)


def slot_table(index):
    columns = jnp.arange(EXPERTS * CAP, dtype=jnp.int32)
    return (columns[:, None] == index[None, :]).astype(jnp.bfloat16)


def fill_slots(table, rows, shards):
    picked = jnp.dot(table, rows, preferred_element_type=jnp.float32).astype(jnp.bfloat16)
    return jnp.repeat(picked.reshape(EXPERTS, CAP, rows.shape[1]), shards, axis=0)


def collect_rows(returned, index, shards):
    width = returned.shape[2]
    summed = (
        returned.reshape(EXPERTS, shards, returned.shape[1], width).astype(jnp.float32).sum(axis=1)
    )
    return jnp.take(summed.reshape(EXPERTS * CAP, width), index, axis=0)


def local(
    fwd_state,
    bwd_state,
    saved_input,
    fwd_route,
    bwd_route,
    fwd_gate,
    bwd_gate,
    w_gate,
    w_up,
    w_down,
    norm_gain,
):
    shards = lax.axis_size("expert") // EXPERTS
    gain = norm_gain[0]
    gate_cols = w_gate[0]
    up_cols = w_up[0]
    down_rows = w_down[0]
    steps_total = fwd_route.shape[1]
    forward = fwd_state[0]
    backward = bwd_state[0]
    new_forward = forward
    new_backward = backward
    for moment in range(steps_total):
        fwd_index = slot_index(fwd_route[0, moment, :, 0])
        fwd_raw, fwd_scale, fwd_norm = norm_rows(forward, gain)
        fwd_slots = fill_slots(slot_table(fwd_index), fwd_norm, shards)
        bwd_index = slot_index(bwd_route[0, moment, :, 0])
        bwd_table = slot_table(bwd_index)
        bwd_raw, bwd_scale, bwd_norm = norm_rows(saved_input[0, moment], gain)
        scaled = (bwd_gate[0, moment][:, None] * backward.astype(jnp.float32)).astype(jnp.bfloat16)
        bwd_inputs = fill_slots(bwd_table, bwd_norm, shards)
        bwd_grads = fill_slots(bwd_table, scaled, shards)
        expert_received = lax.all_to_all(
            fwd_slots, "expert", split_axis=0, concat_axis=0, tiled=True
        )
        expert_gated = jnp.einsum(
            "scd,dh->sch", expert_received, gate_cols, preferred_element_type=jnp.float32
        )
        expert_upped = jnp.einsum(
            "scd,dh->sch", expert_received, up_cols, preferred_element_type=jnp.float32
        )
        hidden = (expert_gated * jax.nn.sigmoid(expert_gated) * expert_upped).astype(jnp.bfloat16)
        fwd_partial = jnp.einsum(
            "sch,hd->scd", hidden, down_rows, preferred_element_type=jnp.float32
        ).astype(jnp.bfloat16)
        fwd_back = lax.all_to_all(fwd_partial, "expert", split_axis=0, concat_axis=0, tiled=True)
        inputs_part = lax.all_to_all(bwd_inputs, "expert", split_axis=0, concat_axis=0, tiled=True)
        grads_part = lax.all_to_all(bwd_grads, "expert", split_axis=0, concat_axis=0, tiled=True)
        gated = jnp.einsum(
            "scd,dh->sch", inputs_part, gate_cols, preferred_element_type=jnp.float32
        )
        upped = jnp.einsum("scd,dh->sch", inputs_part, up_cols, preferred_element_type=jnp.float32)
        dhidden = jnp.einsum(
            "scd,hd->sch", grads_part, down_rows, preferred_element_type=jnp.float32
        )
        sigma = jax.nn.sigmoid(gated)
        dgate = (dhidden * upped * sigma * (1.0 + gated * (1.0 - sigma))).astype(jnp.bfloat16)
        dup = (dhidden * gated * sigma).astype(jnp.bfloat16)
        result = jnp.einsum("sch,dh->scd", dgate, gate_cols, preferred_element_type=jnp.float32)
        result = result + jnp.einsum(
            "sch,dh->scd", dup, up_cols, preferred_element_type=jnp.float32
        )
        bwd_partial = result.astype(jnp.bfloat16)
        bwd_back = lax.all_to_all(bwd_partial, "expert", split_axis=0, concat_axis=0, tiled=True)
        moe_rows = collect_rows(fwd_back, fwd_index, shards)
        new_forward = (fwd_raw + fwd_gate[0, moment][:, None] * moe_rows).astype(jnp.bfloat16)
        dnorm = collect_rows(bwd_back, bwd_index, shards)
        weighted = gain * dnorm
        cubed = bwd_scale * bwd_scale * bwd_scale
        dinput = bwd_scale * weighted - bwd_raw * cubed * jnp.mean(
            bwd_raw * weighted, axis=-1, keepdims=True
        )
        new_backward = (backward.astype(jnp.float32) + dinput).astype(jnp.bfloat16)
        if moment + 1 < steps_total:
            forward = passed_along(new_forward, "pipe", 1)
            backward = passed_along(new_backward, "pipe", -1)
    return (new_forward[None], new_backward[None])


def solution(mesh):
    placed = (
        P("pipe", "expert", None),
        P("pipe", "expert", None),
        P("pipe", None, "expert", None),
        P("pipe", None, "expert", None),
        P("pipe", None, "expert", None),
        P("pipe", None, "expert"),
        P("pipe", None, "expert"),
        P("pipe", None, "expert"),
        P("pipe", None, "expert"),
        P("pipe", "expert", None),
        P("pipe", None),
    )
    return jax.shard_map(
        local,
        mesh=mesh,
        in_specs=placed,
        out_specs=(P("pipe", "expert", None), P("pipe", "expert", None)),
        check_vma=False,
    )
```

profile of v0, /device:TPU:0, one launch (start us, length us, event | category | flops | bytes accessed | tf_op | source)
XLA Modules:
  0.0 158.4 jit_solution(18121276886140860241)
XLA Ops:
  0.6 0.8 slice_bitcast_fusion.1
  1.6 1.1 fusion.42
  3.5 0.7 copy-done.24
  4.8 1.2 convolution_convert_fusion.4
  6.0 0.8 broadcast_in_dim.29
  6.8 5.3 %all-to-all-start.5 = ((bf16[8,7,3584]{2,1,0:T(8,128)(2,1)}), bf16[8,7,3584]{2,1,0:T(8,128)(2,1)S(1)}, u32[]{:S(2)}, u32[]{:S(2)}) async-start(bf16[8,7,3584]{2,1,0:T(8,128)(2,1)} %bitcast.24), calls=%async_computation.5 | async-start | bytes 917504 | tf_op jit(solution)/shard_map/all_to_all | solution.py:96
  12.2 0.7 copy-done.37
  13.4 0.6 pad_clamp_fusion.1
  17.1 0.6 pad_clamp_fusion.3
  17.9 0.6 pad_clamp_fusion.2
  18.5 0.6 slice_bitcast_fusion.5
  19.1 2.1 %all-to-all-done.5 = bf16[8,7,3584]{2,1,0:T(8,128)(2,1)S(1)} async-done(((bf16[8,7,3584]{2,1,0:T(8,128)(2,1)}), bf16[8,7,3584]{2,1,0:T(8,128)(2,1)S(1)}, u32[]{:S(2)}, u32[]{:S(2)}) %all-to-all-start.5) | async-done | bytes 401440 | tf_op jit(solution)/shard_map/all_to_all | solution.py:96
  21.2 0.8 broadcast_in_dim.28
  22.0 3.5 %all-to-all-start.4 = ((bf16[8,7,3584]{2,1,0:T(8,128)(2,1)}), bf16[8,7,3584]{2,1,0:T(8,128)(2,1)S(1)}, u32[]{:S(2)}, u32[]{:S(2)}) async-start(bf16[8,7,3584]{2,1,0:T(8,128)(2,1)} %bitcast.22), calls=%async_computation.4 | async-start | bytes 917504 | tf_op jit(solution)/shard_map/all_to_all | solution.py:97
  26.1 8.3 %all-to-all-done.4 = bf16[8,7,3584]{2,1,0:T(8,128)(2,1)S(1)} async-done(((bf16[8,7,3584]{2,1,0:T(8,128)(2,1)}), bf16[8,7,3584]{2,1,0:T(8,128)(2,1)S(1)}, u32[]{:S(2)}, u32[]{:S(2)}) %all-to-all-start.4) | async-done | bytes 401440 | tf_op jit(solution)/shard_map/all_to_all | solution.py:97
  34.4 0.8 broadcast_in_dim.25
  35.3 3.5 %all-to-all-start = ((bf16[8,7,3584]{2,1,0:T(8,128)(2,1)}), bf16[8,7,3584]{2,1,0:T(8,128)(2,1)S(1)}, u32[]{:S(2)}, u32[]{:S(2)}) async-start(bf16[8,7,3584]{2,1,0:T(8,128)(2,1)} %bitcast.131), calls=%async_computation | async-start | bytes 917504 | tf_op jit(solution)/shard_map/all_to_all | solution.py:82
  38.8 1.5 fusion.4
  41.2 0.9 copy.38
  42.1 5.7 %all-to-all-done = bf16[8,7,3584]{2,1,0:T(8,128)(2,1)S(1)} async-done(((bf16[8,7,3584]{2,1,0:T(8,128)(2,1)}), bf16[8,7,3584]{2,1,0:T(8,128)(2,1)S(1)}, u32[]{:S(2)}, u32[]{:S(2)}) %all-to-all-start) | async-done | bytes 401440 | tf_op jit(solution)/shard_map/all_to_all | solution.py:82
  47.8 4.1 %all-to-all-start.6 = ((bf16[8,7,3584]{2,1,0:T(8,128)(2,1)}), bf16[8,7,3584]{2,1,0:T(8,128)(2,1)}, u32[]{:S(2)}, u32[]{:S(2)}) async-start(bf16[8,7,3584]{2,1,0:T(8,128)(2,1)} %copy.38), calls=%async_computation.6 | async-start | bytes 917504 | tf_op jit(solution)/shard_map/all_to_all | solution.py:113
  52.8 0.9 copy.27
  53.7 7.2 %all-to-all-done.6 = bf16[8,7,3584]{2,1,0:T(8,128)(2,1)} async-done(((bf16[8,7,3584]{2,1,0:T(8,128)(2,1)}), bf16[8,7,3584]{2,1,0:T(8,128)(2,1)}, u32[]{:S(2)}, u32[]{:S(2)}) %all-to-all-start.6) | async-done | bytes 401440 | tf_op jit(solution)/shard_map/all_to_all | solution.py:113
  60.9 4.1 %all-to-all-start.1 = ((bf16[8,7,3584]{2,1,0:T(8,128)(2,1)}), bf16[8,7,3584]{2,1,0:T(8,128)(2,1)}, u32[]{:S(2)}, u32[]{:S(2)}) async-start(bf16[8,7,3584]{2,1,0:T(8,128)(2,1)} %copy.27), calls=%async_computation.1 | async-start | bytes 917504 | tf_op jit(solution)/shard_map/all_to_all | solution.py:95
  65.0 1.9 %convert_reduce_fusion.1 = f32[4,7,3584]{2,1,0:T(8,128)} fusion(bf16[8,7,3584]{2,1,0:T(8,128)(2,1)} %all-to-all-done.6), kind=kLoop, calls=%fused_computation.17 | loop fusion | flops 301056 | bytes 802816 | tf_op jit(solution)/shard_map/reduce_sum | solution.py:44
  67.0 1.1 reshape.179
  68.1 1.7 %gather_fusion.2 = f32[24,3584]{1,0:T(8,128)} fusion(f32[28,3584]{1,0:T(8,128)S(1)} %reshape.179, s32[1024]{0:T(1024)} %pad_clamp_fusion.1), kind=kCustom, calls=%fused_computation.2.clone | custom fusion | bytes 688224 | tf_op jit(solution)/shard_map/jit(_take)/gather | solution.py:46
  69.7 0.6 copy-done.22
  70.3 1.3 fusion.47
  72.3 0.9 fusion.33
  73.1 1.3 collective-permute-start.1
  76.0 0.8 broadcast_in_dim.31
  76.8 4.1 %all-to-all-start.8 = ((bf16[8,7,3584]{2,1,0:T(8,128)(2,1)}), bf16[8,7,3584]{2,1,0:T(8,128)(2,1)}, u32[]{:S(2)}, u32[]{:S(2)}) async-start(bf16[8,7,3584]{2,1,0:T(8,128)(2,1)} %bitcast.31), calls=%async_computation.8 | async-start | bytes 917504 | tf_op jit(solution)/shard_map/all_to_all | solution.py:96
  80.9 1.9 %convert_reduce_fusion.3 = f32[4,7,3584]{2,1,0:T(8,128)} fusion(bf16[8,7,3584]{2,1,0:T(8,128)(2,1)} %all-to-all-done.1), kind=kLoop, calls=%fused_computation.19 | loop fusion | flops 301056 | bytes 802816 | tf_op jit(solution)/shard_map/reduce_sum | solution.py:44
  82.9 1.1 reshape.171
  83.9 1.5 gather_fusion
  85.5 0.7 copy-done.34
  86.1 1.8 %fusion.41 = bf16[24,3584]{1,0:T(8,128)(2,1)} fusion(f32[24,3584]{1,0:T(8,128)} %gather_fusion, bf16[1,24,3584]{2,1,0:T(8,128)(2,1)} %param.13, f32[24]{0:T(128)S(1)} %copy-done.34, pred[24]{0:T(512)(128)(4,1)S(1)} %copy-done.36), kind=kLoop, calls=%fused_computation.77 | loop fusion | flops 430080 | bytes 688248 | tf_op jit(solution)/shard_map/convert_element_type | solution.py:115
  88.0 4.7 %collective-permute-start = (bf16[24,3584]{1,0:T(8,128)(2,1)}, bf16[24,3584]{1,0:T(8,128)(2,1)S(1)}, u32[]{:S(2)}, u32[]{:S(2)}) collective-permute-start(bf16[24,3584]{1,0:T(8,128)(2,1)} %fusion.41), channel_id=1, source_target_pairs={{0,8},{8,16},{16,24},{1,9},{9,17},{17,25},{2,10},{10,18},{18,26},{... | collective-permute-start | bytes 516104 | tf_op jit(solution)/shard_map/ppermute | solution.py:16
  92.7 1.2 convolution_convert_fusion.3
  93.9 0.8 reshape.180
  94.6 2.6 %collective-permute-done = bf16[24,3584]{1,0:T(8,128)(2,1)S(1)} collective-permute-done((bf16[24,3584]{1,0:T(8,128)(2,1)}, bf16[24,3584]{1,0:T(8,128)(2,1)S(1)}, u32[]{:S(2)}, u32[]{:S(2)}) %collective-permute-start) | collective-permute-done | bytes 172064 | tf_op jit(solution)/shard_map/ppermute | solution.py:16
  98.2 0.8 reshape.172
  99.0 1.7 %broadcast_in_dim.30 = bf16[4,2,7,3584]{3,2,1,0:T(8,128)(2,1)} broadcast(bf16[4,7,3584]{2,1,0:T(8,128)(2,1)} %reshape.180), dimensions={0,2,3} | broadcast | bytes 602112 | tf_op jit(solution)/shard_map/broadcast_in_dim | solution.py:38
  100.7 3.8 %all-to-all-start.7 = ((bf16[8,7,3584]{2,1,0:T(8,128)(2,1)}), bf16[8,7,3584]{2,1,0:T(8,128)(2,1)S(1)}, u32[]{:S(2)}, u32[]{:S(2)}) async-start(bf16[8,7,3584]{2,1,0:T(8,128)(2,1)} %bitcast.133), calls=%async_computation.7 | async-start | bytes 917504 | tf_op jit(solution)/shard_map/all_to_all | solution.py:97
  104.5 1.9 %fusion.20 = f32[8,7,128]{2,1,0:T(8,128)} fusion(bf16[8,7,3584]{2,1,0:T(8,128)(2,1)} %all-to-all-done.8, bf16[1,3584,128]{2,1,0:T(8,128)(2,1)S(1)} %copy-done.1), kind=kOutput, calls=%fused_computation.38 | convolution fusion | flops 51380224 | bytes 1347584 | tf_op jit(solution)/shard_map/scd,dh->sch/dot_general | solution.py:98
  106.5 2.0 %fusion.9 = f32[8,7,128]{2,1,0:T(8,128)} fusion(bf16[8,7,3584]{2,1,0:T(8,128)(2,1)} %all-to-all-done.8, bf16[1,3584,128]{2,1,0:T(8,128)(2,1)S(1)} %copy-done), kind=kOutput, calls=%fused_computation.27 | convolution fusion | flops 51380224 | bytes 1347584 | tf_op jit(solution)/shard_map/scd,dh->sch/dot_general | solution.py:101
  108.4 5.1 %all-to-all-done.7 = bf16[8,7,3584]{2,1,0:T(8,128)(2,1)S(1)} async-done(((bf16[8,7,3584]{2,1,0:T(8,128)(2,1)}), bf16[8,7,3584]{2,1,0:T(8,128)(2,1)S(1)}, u32[]{:S(2)}, u32[]{:S(2)}) %all-to-all-start.7) | async-done | bytes 401440 | tf_op jit(solution)/shard_map/all_to_all | solution.py:97
  113.5 1.9 %broadcast_in_dim.26 = bf16[4,2,7,3584]{3,2,1,0:T(8,128)(2,1)} broadcast(bf16[4,7,3584]{2,1,0:T(8,128)(2,1)} %reshape.172), dimensions={0,2,3} | broadcast | bytes 602112 | tf_op jit(solution)/shard_map/broadcast_in_dim | solution.py:38
  115.5 3.5 %all-to-all-start.2 = ((bf16[8,7,3584]{2,1,0:T(8,128)(2,1)}), bf16[8,7,3584]{2,1,0:T(8,128)(2,1)S(1)}, u32[]{:S(2)}, u32[]{:S(2)}) async-start(bf16[8,7,3584]{2,1,0:T(8,128)(2,1)} %bitcast.132), calls=%async_computation.2 | async-start | bytes 917504 | tf_op jit(solution)/shard_map/all_to_all | solution.py:82
  119.0 1.5 fusion.2
  121.3 0.9 copy.44
  122.2 5.6 %all-to-all-done.2 = bf16[8,7,3584]{2,1,0:T(8,128)(2,1)S(1)} async-done(((bf16[8,7,3584]{2,1,0:T(8,128)(2,1)}), bf16[8,7,3584]{2,1,0:T(8,128)(2,1)S(1)}, u32[]{:S(2)}, u32[]{:S(2)}) %all-to-all-start.2) | async-done | bytes 401440 | tf_op jit(solution)/shard_map/all_to_all | solution.py:82
  127.9 4.1 %all-to-all-start.9 = ((bf16[8,7,3584]{2,1,0:T(8,128)(2,1)}), bf16[8,7,3584]{2,1,0:T(8,128)(2,1)}, u32[]{:S(2)}, u32[]{:S(2)}) async-start(bf16[8,7,3584]{2,1,0:T(8,128)(2,1)} %copy.44), calls=%async_computation.9 | async-start | bytes 917504 | tf_op jit(solution)/shard_map/all_to_all | solution.py:113
  132.9 0.9 copy.32
  133.8 7.2 %all-to-all-done.9 = bf16[8,7,3584]{2,1,0:T(8,128)(2,1)} async-done(((bf16[8,7,3584]{2,1,0:T(8,128)(2,1)}), bf16[8,7,3584]{2,1,0:T(8,128)(2,1)}, u32[]{:S(2)}, u32[]{:S(2)}) %all-to-all-start.9) | async-done | bytes 401440 | tf_op jit(solution)/shard_map/all_to_all | solution.py:113
  141.0 3.5 %all-to-all-start.3 = ((bf16[8,7,3584]{2,1,0:T(8,128)(2,1)}), bf16[8,7,3584]{2,1,0:T(8,128)(2,1)S(1)}, u32[]{:S(2)}, u32[]{:S(2)}) async-start(bf16[8,7,3584]{2,1,0:T(8,128)(2,1)} %copy.32), calls=%async_computation.3 | async-start | bytes 917504 | tf_op jit(solution)/shard_map/all_to_all | solution.py:95
  144.5 1.2 convert_reduce_fusion
  145.8 0.9 gather_fusion.3
  147.5 5.9 %all-to-all-done.3 = bf16[8,7,3584]{2,1,0:T(8,128)(2,1)S(1)} async-done(((bf16[8,7,3584]{2,1,0:T(8,128)(2,1)}), bf16[8,7,3584]{2,1,0:T(8,128)(2,1)S(1)}, u32[]{:S(2)}, u32[]{:S(2)}) %all-to-all-start.3) | async-done | bytes 401440 | tf_op jit(solution)/shard_map/all_to_all | solution.py:95
  153.6 0.8 gather_fusion.1
  155.1 1.8 %fusion.60 = bf16[1,24,3584]{2,1,0:T(8,128)(2,1)} fusion(f32[24,3584]{1,0:T(8,128)S(1)} %gather_fusion.3, bf16[24,3584]{1,0:T(8,128)(2,1)} %collective-permute-done.1, f32[24]{0:T(128)S(1)} %broadcast_multiply_fusion, f32[24]{0:T(128)S(1)} %copy-done.40, f32[24]{0:T(128)S(1)} %copy-done.32, f32[3584]{0:T(1024)S(1)} %copy-done.13, ...), kind=kLoop, calls=%fused_computation.95 | loop fusion | flops 860160 | bytes 874808 | tf_op jit(solution)/shard_map/broadcast_in_dim | solution.py:126
  156.9 0.7 copy-done.33
  157.6 0.8 fusion.57
  (132 shorter events, 14.6 us)
Async XLA Ops:
  0.6 25.2 %copy-start = (bf16[1,3584,128]{2,1,0:T(8,128)(2,1)S(1)}, bf16[1,3584,128]{2,1,0:T(8,128)(2,1)}, u32[]{:S(2)}) copy-start(bf16[1,3584,128]{2,1,0:T(8,128)(2,1)} %param.21) | copy-start | bytes 2752516
  3.3 1.5 copy-start.29
  3.3 1.4 copy-start.18
  3.5 0.7 copy-start.24
  4.7 9.3 %copy-start.19 = (s32[24]{0:T(128)}, s32[24]{0:T(128)S(1)}, u32[]{:S(2)}) copy-start(s32[24]{0:T(128)S(1)} %get-tuple-element.6) | copy-start | bytes 292
  4.7 11.2 %copy-start.10 = (f32[3584]{0:T(1024)}, f32[3584]{0:T(1024)S(1)}, u32[]{:S(2)}) copy-start(f32[3584]{0:T(1024)S(1)} %reduce) | copy-start | bytes 43012
  6.8 8.1 %copy-start.9 = (bf16[1,24,3584]{2,1,0:T(8,128)(2,1)S(1)}, bf16[1,24,3584]{2,1,0:T(8,128)(2,1)}, u32[]{:S(2)}) copy-start(bf16[1,24,3584]{2,1,0:T(8,128)(2,1)} %param.13) | copy-start | bytes 516100
  6.8 14.3 %all-to-all-start.5 = ((bf16[8,7,3584]{2,1,0:T(8,128)(2,1)}), bf16[8,7,3584]{2,1,0:T(8,128)(2,1)S(1)}, u32[]{:S(2)}, u32[]{:S(2)}) async-start(bf16[8,7,3584]{2,1,0:T(8,128)(2,1)} %bitcast.24), calls=%async_computation.5 | async-start | bytes 917504 | tf_op jit(solution)/shard_map/all_to_all | solution.py:96
  12.2 0.7 copy-start.37
  14.0 0.7 copy-start.25
  15.9 0.5 copy-start.27
  15.9 0.9 copy-start.14
  17.8 0.7 copy-start.38
  17.9 7.6 %copy-start.1 = (bf16[1,3584,128]{2,1,0:T(8,128)(2,1)S(1)}, bf16[1,3584,128]{2,1,0:T(8,128)(2,1)}, u32[]{:S(2)}) copy-start(bf16[1,3584,128]{2,1,0:T(8,128)(2,1)} %param.20) | copy-start | bytes 2752516
  22.0 12.4 %all-to-all-start.4 = ((bf16[8,7,3584]{2,1,0:T(8,128)(2,1)}), bf16[8,7,3584]{2,1,0:T(8,128)(2,1)S(1)}, u32[]{:S(2)}, u32[]{:S(2)}) async-start(bf16[8,7,3584]{2,1,0:T(8,128)(2,1)} %bitcast.22), calls=%async_computation.4 | async-start | bytes 917504 | tf_op jit(solution)/shard_map/all_to_all | solution.py:97
  26.1 12.7 %copy-start.2 = (bf16[1,128,3584]{2,1,0:T(8,128)(2,1)S(1)}, bf16[1,128,3584]{2,1,0:T(8,128)(2,1)}, u32[]{:S(2)}) copy-start(bf16[1,128,3584]{2,1,0:T(8,128)(2,1)} %param.22) | copy-start | bytes 2752516
  34.4 0.9 copy-start.5
  35.3 12.4 %all-to-all-start = ((bf16[8,7,3584]{2,1,0:T(8,128)(2,1)}), bf16[8,7,3584]{2,1,0:T(8,128)(2,1)S(1)}, u32[]{:S(2)}, u32[]{:S(2)}) async-start(bf16[8,7,3584]{2,1,0:T(8,128)(2,1)} %bitcast.131), calls=%async_computation | async-start | bytes 917504 | tf_op jit(solution)/shard_map/all_to_all | solution.py:82
  47.8 13.2 %all-to-all-start.6 = ((bf16[8,7,3584]{2,1,0:T(8,128)(2,1)}), bf16[8,7,3584]{2,1,0:T(8,128)(2,1)}, u32[]{:S(2)}, u32[]{:S(2)}) async-start(bf16[8,7,3584]{2,1,0:T(8,128)(2,1)} %copy.38), calls=%async_computation.6 | async-start | bytes 917504 | tf_op jit(solution)/shard_map/all_to_all | solution.py:113
  60.9 15.1 %all-to-all-start.1 = ((bf16[8,7,3584]{2,1,0:T(8,128)(2,1)}), bf16[8,7,3584]{2,1,0:T(8,128)(2,1)}, u32[]{:S(2)}, u32[]{:S(2)}) async-start(bf16[8,7,3584]{2,1,0:T(8,128)(2,1)} %copy.27), calls=%async_computation.1 | async-start | bytes 917504 | tf_op jit(solution)/shard_map/all_to_all | solution.py:95
  68.0 1.7 %copy-start.3 = (bf16[1,2,24,3584]{3,2,1,0:T(8,128)(2,1)S(1)}, bf16[1,2,24,3584]{3,2,1,0:T(8,128)(2,1)}, u32[]{:S(2)}) copy-start(bf16[1,2,24,3584]{3,2,1,0:T(8,128)(2,1)} %param.15) | copy-start | bytes 1032196
  69.7 0.6 copy-start.22
  70.3 1.3 copy-start.4
  70.3 1.3 copy-start.11
  70.3 1.3 copy-start.15
  71.6 0.6 copy-start.30
  71.6 0.7 copy-start.39
  73.1 19.5 %collective-permute-start.1 = (bf16[24,3584]{1,0:T(8,128)(2,1)}, bf16[24,3584]{1,0:T(8,128)(2,1)}, u32[]{:S(2)}, u32[]{:S(2)}) collective-permute-start(bf16[24,3584]{1,0:T(8,128)(2,1)} %fusion.33), channel_id=1, source_target_pairs={{8,0},{16,8},{24,16},{9,1},{17,9},{25,17},{10,2},{18,10},{26,18},{... | collective-permute-start | bytes 516104 | tf_op jit(solution)/shard_map/ppermute | solution.py:16
  75.0 0.5 copy-start.31
  75.0 0.6 copy-start.20
  76.8 22.2 %all-to-all-start.8 = ((bf16[8,7,3584]{2,1,0:T(8,128)(2,1)}), bf16[8,7,3584]{2,1,0:T(8,128)(2,1)}, u32[]{:S(2)}, u32[]{:S(2)}) async-start(bf16[8,7,3584]{2,1,0:T(8,128)(2,1)} %bitcast.31), calls=%async_computation.8 | async-start | bytes 917504 | tf_op jit(solution)/shard_map/all_to_all | solution.py:96
  85.5 0.7 copy-start.34
  85.5 0.7 copy-start.36
  88.0 4.7 %copy-start.21 = (s32[24]{0:T(128)S(1)}, s32[24]{0:T(128)}, u32[]{:S(2)}) copy-start(s32[24]{0:T(128)} %copy-done.19) | copy-start | bytes 292
  88.0 4.7 %copy-start.26 = (f32[24]{0:T(128)S(1)}, f32[24]{0:T(128)}, u32[]{:S(2)}) copy-start(f32[24]{0:T(128)} %get-tuple-element.13) | copy-start | bytes 292
  88.0 9.2 %collective-permute-start = (bf16[24,3584]{1,0:T(8,128)(2,1)}, bf16[24,3584]{1,0:T(8,128)(2,1)S(1)}, u32[]{:S(2)}, u32[]{:S(2)}) collective-permute-start(bf16[24,3584]{1,0:T(8,128)(2,1)} %fusion.41), channel_id=1, source_target_pairs={{0,8},{8,16},{16,24},{1,9},{9,17},{17,25},{2,10},{10,18},{18,26},{... | collective-permute-start | bytes 516104 | tf_op jit(solution)/shard_map/ppermute | solution.py:16
  94.6 2.7 %copy-start.12 = (f32[3584]{0:T(1024)S(1)}, f32[3584]{0:T(1024)}, u32[]{:S(2)}) copy-start(f32[3584]{0:T(1024)} %copy-done.10) | copy-start | bytes 43012
  97.2 1.0 copy-start.7
  97.4 0.6 copy-start.28
  100.7 12.8 %all-to-all-start.7 = ((bf16[8,7,3584]{2,1,0:T(8,128)(2,1)}), bf16[8,7,3584]{2,1,0:T(8,128)(2,1)S(1)}, u32[]{:S(2)}, u32[]{:S(2)}) async-start(bf16[8,7,3584]{2,1,0:T(8,128)(2,1)} %bitcast.133), calls=%async_computation.7 | async-start | bytes 917504 | tf_op jit(solution)/shard_map/all_to_all | solution.py:97
  113.5 1.9 %copy-start.6 = (bf16[8,7,3584]{2,1,0:T(8,128)(2,1)}, bf16[8,7,3584]{2,1,0:T(8,128)(2,1)S(1)}, u32[]{:S(2)}) copy-start(bf16[8,7,3584]{2,1,0:T(8,128)(2,1)S(1)} %all-to-all-done.7) | copy-start | bytes 1204228
  115.5 12.4 %all-to-all-start.2 = ((bf16[8,7,3584]{2,1,0:T(8,128)(2,1)}), bf16[8,7,3584]{2,1,0:T(8,128)(2,1)S(1)}, u32[]{:S(2)}, u32[]{:S(2)}) async-start(bf16[8,7,3584]{2,1,0:T(8,128)(2,1)} %bitcast.132), calls=%async_computation.2 | async-start | bytes 917504 | tf_op jit(solution)/shard_map/all_to_all | solution.py:82
  118.9 1.5 copy-start.16
  118.9 1.5 copy-start.17
  127.9 13.2 %all-to-all-start.9 = ((bf16[8,7,3584]{2,1,0:T(8,128)(2,1)}), bf16[8,7,3584]{2,1,0:T(8,128)(2,1)}, u32[]{:S(2)}, u32[]{:S(2)}) async-start(bf16[8,7,3584]{2,1,0:T(8,128)(2,1)} %copy.44), calls=%async_computation.9 | async-start | bytes 917504 | tf_op jit(solution)/shard_map/all_to_all | solution.py:113
  141.0 12.4 %all-to-all-start.3 = ((bf16[8,7,3584]{2,1,0:T(8,128)(2,1)}), bf16[8,7,3584]{2,1,0:T(8,128)(2,1)S(1)}, u32[]{:S(2)}, u32[]{:S(2)}) async-start(bf16[8,7,3584]{2,1,0:T(8,128)(2,1)} %copy.32), calls=%async_computation.3 | async-start | bytes 917504 | tf_op jit(solution)/shard_map/all_to_all | solution.py:95
  145.7 1.0 copy-start.13
  146.7 0.6 copy-start.23
  154.4 0.6 copy-start.32
  154.4 0.7 copy-start.40
  155.1 1.8 %copy-start.8 = (bf16[24,3584]{1,0:T(8,128)(2,1)S(1)}, bf16[24,3584]{1,0:T(8,128)(2,1)}, u32[]{:S(2)}) copy-start(bf16[24,3584]{1,0:T(8,128)(2,1)} %copy-done.7) | copy-start | bytes 516100
  156.9 0.7 copy-start.33
  156.9 0.7 copy-start.35
where the time goes:
time: 160 us; the launch traced here: 158 us
  waiting for transfers between devices  49.7 us (31%)
  starting transfers between devices  45.5 us (28%)
  local copies, waits for them, and re-layouts  28.6 us (18%)
  other arithmetic  18.8 us (12%)
  matrix products  14.5 us (9%)
    all_to_all x2, waiting for transfers between devices, local(): lax.all_to_all(bwd_partial, 'expert', split_axis=0, concat_axis=0, tiled=...  14.4 us
    all_to_all x2, waiting for transfers between devices, local(): lax.all_to_all(bwd_grads, 'expert', split_axis=0, concat_axis=0, tiled=True)  13.4 us
    all_to_all x2, waiting for transfers between devices, local(): lax.all_to_all(fwd_slots, 'expert', split_axis=0, concat_axis=0, tiled=True)  11.3 us
    all_to_all x2, starting transfers between devices, local(): lax.all_to_all(bwd_inputs, 'expert', split_axis=0, concat_axis=0, tiled=T...  9.46 us
    all_to_all x2, starting transfers between devices, local(): lax.all_to_all(bwd_partial, 'expert', split_axis=0, concat_axis=0, tiled=...  8.24 us
    all_to_all x2, starting transfers between devices, local(): lax.all_to_all(fwd_partial, 'expert', split_axis=0, concat_axis=0, tiled=...  7.59 us
    all_to_all x2, starting transfers between devices, local(): lax.all_to_all(bwd_grads, 'expert', split_axis=0, concat_axis=0, tiled=True)  7.28 us
    unnamed x82, local copies, waits for them, and re-layouts  7.25 us
  transfers between devices with their start and end apart: 12, of which 9 were waited for; matrix products, arithmetic and copies ran while one was open for 26% of the time, Pallas kernels for 0%

commit v1 on v0

--- a/solution.py
+++ b/solution.py
@@ -1,13 +1,337 @@
+import functools
+
 import jax
 import jax.numpy as jnp
 from jax import lax
+from jax.experimental import pallas as pl
+from jax.experimental.pallas import tpu as pltpu
 from jax.sharding import PartitionSpec as P
 
 EXPERTS = 4
 CAP = 7
-
-
 EPS = 1e-06
+
+
+SLOT = -(-CAP // 8) * 8
+LANES = 128
+F32 = jnp.float32
+BF16 = jnp.bfloat16
+
+
+def call(body, outs, args, vmem=16, **more):
+    return pl.pallas_call(
+        body,
+        out_shape=outs,
+        compiler_params=pltpu.CompilerParams(vmem_limit_bytes=vmem * 2**20),
+        **more,
+    )(*args)
+
+
+def place():
+    device = lax.axis_index("expert")
+    return device // 2, device % 2
+
+
+def swap_cores(array):
+    pairs = [(i, i ^ 1) for i in range(lax.axis_size("expert"))]
+    return lax.ppermute(array, "expert", pairs)
+
+
+def exchange(pieces):
+    moved = [pieces[0]]
+    for m in range(1, EXPERTS):
+        pairs = [(i, i ^ (2 * m)) for i in range(lax.axis_size("expert"))]
+        moved.append(lax.ppermute(pieces[m], "expert", pairs))
+    return moved
+
+
+def swap_ranks(array, first):
+    ranks_total, devices = lax.axis_size("pipe"), lax.axis_size("expert")
+    target = [i ^ 2 for i in range(ranks_total * devices)]
+    for rank in range(first, ranks_total - 1, 2):
+        for i in range(devices):
+            a, b = rank * devices + i, (rank + 1) * devices + i
+            target[a], target[b] = b, a
+    return lax.ppermute(array, ("pipe", "expert"), list(enumerate(target)))
+
+
+def slot_of(rows, line, tokens, axis):
+    chip, _ = place()
+    row, col = rows[line : line + 1, :tokens], rows.T[:tokens, line : line + 1]
+    down = lax.broadcasted_iota(jnp.int32, (tokens, tokens), 0)
+    across = lax.broadcasted_iota(jnp.int32, (tokens, tokens), 1)
+    earlier = down < across if axis == 0 else across < down
+    rank = jnp.sum(jnp.where((row == col) & earlier, 1, 0), axis=axis, keepdims=True)
+    route = (row if axis == 0 else col).astype(jnp.int32)
+    return (route ^ chip) * SLOT + rank
+
+
+def table_to_slots(rows, line, tokens, wanted=True):
+    down = lax.broadcasted_iota(jnp.int32, (EXPERTS * SLOT, tokens), 0)
+    hit = (down == slot_of(rows, line, tokens, 0)) & wanted
+    return jnp.where(hit, 1.0, 0.0).astype(BF16)
+
+
+def table_to_tokens(rows, line, tokens):
+    across = lax.broadcasted_iota(jnp.int32, (tokens, EXPERTS * SLOT), 1)
+    return jnp.where(across == slot_of(rows, line, tokens, 1), 1.0, 0.0).astype(BF16)
+
+
+def gate_lanes(rows, line, tokens, lane):
+    gate = rows.T[:tokens, line : line + 1]
+    high = gate.astype(BF16).astype(F32)
+    at = lax.broadcasted_iota(jnp.int32, (tokens, LANES), 1) - lane
+    return jnp.where(at == 0, high, jnp.where(at == 1, gate - high, 0.0)).astype(BF16)
+
+
+def placed(table, rows):
+    return jnp.dot(table, rows, preferred_element_type=F32)
+
+
+def put_pieces(outs, at, value):
+    for m, out in enumerate(outs):
+        out[:, at : at + value.shape[1]] = value[m * SLOT : (m + 1) * SLOT].astype(BF16)
+
+
+def put_gates(rows, step, steps, tokens, fwd_table, bwd_table, outs):
+    value = placed(fwd_table, gate_lanes(rows, 2 * steps + step, tokens, 0))
+    value = value + placed(bwd_table, gate_lanes(rows, 3 * steps + step, tokens, 2))
+    put_pieces(outs, 0, value)
+
+
+def first_spread_body(steps, tokens, *refs):
+    small, (state, grad, saved), refs = refs[:4], refs[4:7], refs[7:]
+    lines, outs, scratch, sems = refs[0], refs[1 : 1 + EXPERTS], refs[1 + EXPERTS : -1], refs[-1]
+    width = state.shape[1]
+    sources = [*small, state, grad, saved.at[pl.ds(0, tokens), :]]
+    copies = [
+        pltpu.make_async_copy(src, dst, sems.at[i])
+        for i, (src, dst) in enumerate(zip(sources, scratch))
+    ]
+    for copy in copies:
+        copy.start()
+    lines[...] = jnp.zeros(lines.shape, F32)
+    for i in range(4):
+        copies[i].wait()
+        lines[i * steps : (i + 1) * steps, :tokens] = scratch[i][...].astype(F32)
+    rows = lines[...]
+    fwd_table = table_to_slots(rows, 0, tokens)
+    bwd_table = table_to_slots(rows, steps, tokens)
+    put_gates(rows, 0, steps, tokens, fwd_table, bwd_table, outs)
+    for i, (table, at) in enumerate(((fwd_table, 0), (bwd_table, 1), (bwd_table, 2))):
+        copies[4 + i].wait()
+        put_pieces(outs, LANES + at * width, placed(table, scratch[4 + i][...]))
+
+
+def first_spread(small, state, grad, saved):
+    steps, tokens = small[0].shape
+    width = state.shape[1]
+    outs = [jax.ShapeDtypeStruct((-(-4 * steps // 8) * 8, LANES), F32)]
+    outs += [jax.ShapeDtypeStruct((SLOT, LANES + 3 * width), BF16)] * EXPERTS
+    args = [*small, state, grad, saved]
+    return call(
+        functools.partial(first_spread_body, steps, tokens),
+        outs,
+        [pltpu.with_memory_space_constraint(a, pltpu.HBM) for a in args],
+        in_specs=[pl.BlockSpec(memory_space=pltpu.HBM)] * len(args),
+        scratch_shapes=[pltpu.VMEM((steps, tokens), a.dtype) for a in small]
+        + [pltpu.VMEM((tokens, width), BF16)] * 3
+        + [pltpu.SemaphoreType.DMA((len(args),))],
+    )
+
+
+def spread_saved_body(step, steps, tokens, *refs):
+    lines, saved, outs = refs[0], refs[1], refs[2:]
+    table = table_to_slots(lines[...], steps + step, tokens)
+    put_pieces(outs, 0, placed(table, saved[step * tokens : (step + 1) * tokens, :]))
+
+
+def spread_body(step, steps, tokens, *refs):
+    lines, low, high, outs = refs[0], refs[1], refs[2], refs[3:]
+    width = low.shape[1]
+    rank, last = lax.axis_index("pipe"), lax.axis_size("pipe") - 1
+    even = rank % 2 == 0
+    rows = lines[...]
+    fwd_table = table_to_slots(rows, step, tokens, rank != 0)
+    bwd_table = table_to_slots(rows, steps + step, tokens, rank != last)
+    put_gates(rows, step, steps, tokens, fwd_table, bwd_table, outs)
+
+    def put(forward, backward):
+        put_pieces(outs, LANES, placed(fwd_table, forward[...]))
+        put_pieces(outs, LANES + width, placed(bwd_table, backward[...]))
+
+    pl.when(even)(lambda: put(high, low))
+    pl.when(jnp.logical_not(even))(lambda: put(low, high))
+
+
+def gather_body(step, steps, tokens, last, *refs):
+    lines, pieces, outs = refs[0], refs[1 : 1 + EXPERTS], refs[1 + EXPERTS :]
+    width = outs[0].shape[1]
+    rows = lines[...]
+    even = lax.axis_index("pipe") % 2 == 0
+    for stream, line in enumerate((step, steps + step)):
+        lanes = slice(stream * width, (stream + 1) * width)
+        slots = jnp.concatenate([p[:, lanes] for p in pieces], axis=0)
+        value = placed(table_to_tokens(rows, line, tokens), slots).astype(BF16)
+        if last:
+            outs[stream][...] = value
+            continue
+
+        @pl.when(even)
+        def _():
+            outs[stream][...] = value
+
+        @pl.when(jnp.logical_not(even))
+        def _():
+            outs[1 - stream][...] = value
+
+
+def pack_body(*refs):
+    _, core = place()
+    own, other, (cols_out, rows_out, cols_flip, rows_flip, sems) = refs[:3], refs[3:6], refs[6:]
+    h = own[0].shape[1]
+
+    def targets(j):
+        at = pl.multiple_of((core ^ j) * h, h)
+        return (
+            cols_out.at[:, pl.ds(at, h)],
+            cols_out.at[:, pl.ds(pl.multiple_of(2 * h + at, h), h)],
+            rows_out.at[pl.ds(at, h), :],
+        )
+
+    copies = [
+        pltpu.make_async_copy(src, dst, sems.at[i])
+        for i, (src, dst) in enumerate(zip(own, targets(0)))
+    ]
+    for copy in copies:
+        copy.start()
+
+    def flip(j):
+        at = pl.multiple_of((core ^ j) * h, h)
+        gates, ups, downs = targets(j)
+        cols_flip[pl.ds(at, h), :] = gates[...].T
+        cols_flip[pl.ds(pl.multiple_of(2 * h + at, h), h), :] = ups[...].T
+        rows_flip[:, pl.ds(at, h)] = downs[...].T
+
+    for src, dst in zip(other, targets(1)):
+        dst[...] = src[...]
+    flip(1)
+    for copy in copies:
+        copy.wait()
+    flip(0)
+
+
+def pack(own):
+    width, units = own[0].shape
+    others = [swap_cores(array) for array in own]
+    own = [pltpu.with_memory_space_constraint(array, pltpu.HBM) for array in own]
+    return call(
+        pack_body,
+        [
+            jax.ShapeDtypeStruct((width, 4 * units), BF16),
+            jax.ShapeDtypeStruct((2 * units, width), BF16),
+            jax.ShapeDtypeStruct((4 * units, width), BF16),
+            jax.ShapeDtypeStruct((width, 2 * units), BF16),
+        ],
+        [*own, *others],
+        in_specs=[pl.BlockSpec(memory_space=pltpu.HBM)] * 3
+        + [pl.BlockSpec(memory_space=pltpu.VMEM)] * 3,
+        scratch_shapes=[pltpu.SemaphoreType.DMA((3,))],
+    )
+
+
+def normed_of(rows, gain_ref):
+    values = rows.astype(F32)
+    mean = jnp.mean(values * values, axis=-1, keepdims=True)
+    scale = lax.rsqrt(mean + EPS)
+    return scale, (values * scale * gain_ref[...]).astype(BF16)
+
+
+def expert_body(gain_ref, cols_ref, rows_ref, cols_flip, rows_flip, *refs):
+    pieces, outs = refs[:EXPERTS], refs[len(refs) - EXPERTS :]
+    n, width = rows_ref.shape
+    half = EXPERTS * SLOT
+
+    def lanes(group, at, size):
+        return jnp.concatenate([p[:, at : at + size] for p in group], axis=0)
+
+    gates = lanes(pieces, 0, LANES).astype(F32)
+    state = lanes(pieces, LANES, width)
+    grad = lanes(pieces, LANES + width, width)
+    if len(refs) == 2 * EXPERTS:
+        saved = lanes(pieces, LANES + 2 * width, width)
+    else:
+        saved = lanes(refs[EXPERTS : 2 * EXPERTS], 0, width)
+    _, fwd_normed = normed_of(state, gain_ref)
+    scale, bwd_normed = normed_of(saved, gain_ref)
+    normed = jnp.concatenate([fwd_normed, bwd_normed], axis=0)
+    both = jnp.dot(normed, cols_ref[...], preferred_element_type=F32)
+
+    gated, upped = both[:half, :n], both[:half, n:]
+    hidden = (gated * jax.nn.sigmoid(gated) * upped).astype(BF16)
+    moe = jnp.dot(hidden, rows_ref[...], preferred_element_type=F32)
+    put_pieces(outs, 0, state.astype(F32) + (gates[:, 0:1] + gates[:, 1:2]) * moe)
+
+    gated, upped = both[half:, :n], both[half:, n:]
+    dhidden = jnp.dot(grad, rows_flip[...], preferred_element_type=F32)
+    dhidden = dhidden * (gates[:, 2:3] + gates[:, 3:4])
+    sigma = jax.nn.sigmoid(gated)
+    dgate = (dhidden * upped * sigma * (1.0 + gated * (1.0 - sigma))).astype(BF16)
+    dup = (dhidden * gated * sigma).astype(BF16)
+    dnorm = jnp.dot(
+        jnp.concatenate([dgate, dup], axis=1), cols_flip[...], preferred_element_type=F32
+    )
+    inner = dgate.astype(F32) * gated + dup.astype(F32) * upped
+    mean = jnp.sum(inner, axis=-1, keepdims=True) / width
+    value = grad.astype(F32) + scale * (gain_ref[...] * dnorm)
+    put_pieces(outs, width, value - saved.astype(F32) * (scale * scale * mean))
+
+
+def by_home_core(
+    fwd_state,
+    bwd_state,
+    saved_input,
+    fwd_route,
+    bwd_route,
+    fwd_gate,
+    bwd_gate,
+    w_gate,
+    w_up,
+    w_down,
+    norm_gain,
+):
+    tokens, width = fwd_state.shape[1:]
+    steps = fwd_route.shape[1]
+    saved = saved_input[0].reshape(steps * tokens, width)
+    small = [a.reshape(steps, tokens) for a in (fwd_route, bwd_route, fwd_gate, bwd_gate)]
+    lines, *made = first_spread(small, fwd_state[0], bwd_state[0], saved)
+    made, own = lax.optimization_barrier((made, (w_gate[0], w_up[0], w_down[0])))
+    pieces = exchange(made)
+    weights = pack(own)
+    one = [jax.ShapeDtypeStruct((SLOT, width), BF16)] * EXPERTS
+    two = [jax.ShapeDtypeStruct((SLOT, 2 * width), BF16)] * EXPERTS
+    main = [jax.ShapeDtypeStruct((SLOT, LANES + 2 * width), BF16)] * EXPERTS
+    state = [jax.ShapeDtypeStruct((tokens, width), BF16)] * 2
+    later = []
+    for step in range(1, steps):
+        body = functools.partial(spread_saved_body, step, steps, tokens)
+        later.append(call(body, one, [lines, saved]))
+    weights, later = lax.optimization_barrier((weights, later))
+    for step in range(steps):
+        back = call(expert_body, two, [norm_gain, *weights, *pieces])
+        last = step + 1 == steps
+        back = exchange(back)
+        body = functools.partial(gather_body, step, steps, tokens, last)
+        made = call(body, state, [lines, *back])
+        if last:
+            return made[0][None], made[1][None]
+        made, ahead = lax.optimization_barrier((made, later[step]))
+        high = swap_ranks(made[1], 1)
+        low = swap_ranks(made[0], 0)
+        ahead = exchange(ahead)
+        body = functools.partial(spread_body, step + 1, steps, tokens)
+        made = call(body, main, [lines, low, high])
+        pieces = exchange(made) + ahead
 
 
 def passed_along(array, axis, by):
@@ -46,7 +370,7 @@
     return jnp.take(summed.reshape(EXPERTS * CAP, width), index, axis=0)
 
 
-def local(
+def by_all_to_all(
     fwd_state,
     bwd_state,
     saved_input,
@@ -71,7 +395,7 @@
     new_backward = backward
     for moment in range(steps_total):
         fwd_index = slot_index(fwd_route[0, moment, :, 0])
-        fwd_raw, fwd_scale, fwd_norm = norm_rows(forward, gain)
+        fwd_raw, _, fwd_norm = norm_rows(forward, gain)
         fwd_slots = fill_slots(slot_table(fwd_index), fwd_norm, shards)
         bwd_index = slot_index(bwd_route[0, moment, :, 0])
         bwd_table = slot_table(bwd_index)
@@ -126,8 +450,14 @@
     return (new_forward[None], new_backward[None])
 
 
+def local(*args):
+    if lax.axis_size("expert") == 2 * EXPERTS:
+        return by_home_core(*args)
+    return by_all_to_all(*args)
+
+
 def solution(mesh):
-    placed = (
+    specs = (
         P("pipe", "expert", None),
         P("pipe", "expert", None),
         P("pipe", None, "expert", None),
@@ -143,7 +473,7 @@
     return jax.shard_map(
         local,
         mesh=mesh,
-        in_specs=placed,
+        in_specs=specs,
         out_specs=(P("pipe", "expert", None), P("pipe", "expert", None)),
         check_vma=False,
     )

time: 160 us -> 61.3 us (0.38)
  local copies, waits for them, and re-layouts: 28.6 us -> 0.98 us
  waiting for transfers between devices: 49.7 us -> 22.7 us
  starting transfers between devices: 45.5 us -> 23.9 us
  other arithmetic: 18.8 us -> 0 us
  matrix products: 14.5 us -> 0 us
  Pallas kernels: 0 us -> 12.7 us
    all_to_all x10 -> x0, waiting for transfers between devices: 47.1 us -> none  [the longest x2 14.4 us: local(): lax.all_to_all(bwd_partial, 'expert', split_axis=0, concat_axis=0, tiled=...]
    all_to_all x10 -> x0, starting transfers between devices: 39.5 us -> none  [the longest x2 9.46 us: local(): lax.all_to_all(bwd_inputs, 'expert', split_axis=0, concat_axis=0, tiled=T...]
    ppermute x2 -> x20, waiting for transfers between devices: 2.57 us -> 22.7 us  [the longest x15 18.5 us: exchange(): moved.append(lax.ppermute(pieces[m], 'expert', pairs))]
    ppermute x2 -> x20, starting transfers between devices: 5.96 us -> 23.9 us  [the longest x15 20.1 us: exchange(): moved.append(lax.ppermute(pieces[m], 'expert', pairs))]
    dot_general x22 -> x0, matrix products: 14.5 us -> none  [the longest x6 3.47 us: fill_slots(): jnp.dot(table, rows, preferred_element_type=jnp.float32)]
    pallas_call x0 -> x8, Pallas kernels: none -> 12.7 us  [call(): pl.pallas_call(body, out_shape=outs, compiler_params=pltpu.CompilerParams...]
    reduce_sum x11 -> x0, other arithmetic: 8.37 us -> none  [the longest x4 5.12 us: collect_rows(): returned.reshape(EXPERTS, shards, returned.shape[1], width)]
    broadcast_in_dim x6 -> x0, local copies, waits for them, and re-layouts: 6.88 us -> none  [fill_slots(): jnp.repeat(picked.reshape(EXPERTS, CAP, rows.shape[1]), shards, axis=0)]
  transfers between devices with their start and end apart: 12 -> 20, of which waited for: 9 -> 10; matrix products, arithmetic and copies ran while one was open for 26% -> 0% of each run, Pallas kernels for 0% -> 5%
where the time goes in v1:
time: 61.3 us; the launch traced here: 61.1 us
  starting transfers between devices  23.9 us (39%)
  waiting for transfers between devices  22.7 us (37%)
  Pallas kernels  12.7 us (21%)
  local copies, waits for them, and re-layouts  0.98 us (2%)
  between operations  0.74 us (1%)
    ppermute x15, starting transfers between devices, exchange(): moved.append(lax.ppermute(pieces[m], 'expert', pairs))  20.1 us
    ppermute x15, waiting for transfers between devices, exchange(): moved.append(lax.ppermute(pieces[m], 'expert', pairs))  18.5 us
    pallas_call x8, Pallas kernels, call(): pl.pallas_call(body, out_shape=outs, compiler_params=pltpu.CompilerParams...  12.7 us
    ppermute x2, waiting for transfers between devices, swap_ranks(): return lax.ppermute(array, ('pipe', 'expert'), list(enumerate(target)))  4.24 us
    ppermute x2, starting transfers between devices, swap_ranks(): return lax.ppermute(array, ('pipe', 'expert'), list(enumerate(target)))  2.8 us
  transfers between devices with their start and end apart: 20, of which 10 were waited for; matrix products, arithmetic and copies ran while one was open for 0% of the time, Pallas kernels for 5%

profile of v1, /device:TPU:0, one launch (start us, length us, event | category | flops | bytes accessed | tf_op | source)
XLA Modules:
  0.0 61.1 jit_solution(10404848888438171057)
XLA Ops:
  0.6 0.0 copy-start.1
  0.6 1.7 %shard_map.122 = (f32[8,128]{1,0:T(8,128)S(1)}, bf16[8,10880]{1,0:T(8,128)(2,1)S(1)}, bf16[8,10880]{1,0:T(8,128)(2,1)S(1)}, bf16[8,10880]{1,0:T(8,128)(2,1)S(1)}, bf16[8,10880]{1,0:T(8,128)(2,1)S(1)}) custom-call(s32[2,24]{1,0:T(2,128)} %bitcast.22, s32[2,24]{1,0:T(2,128)} %bitcast.23, f32[2,24]{1,0:T(2,128)} %bitcast.24, f32[2,24]{1,0:T(2,128)} %bitcast.25, ...), custom_call_target="tpu_custom_call" | custom-call | tf_op jit(solution)/shard_map/pallas_call | solution.py:22
  2.3 0.6 collective-permute-start
  2.9 0.1 collective-permute-start.1
  3.0 0.4 collective-permute-start.2
  3.4 2.6 %collective-permute-start.3 = (bf16[8,10880]{1,0:T(8,128)(2,1)S(1)}, bf16[8,10880]{1,0:T(8,128)(2,1)S(1)}, u32[]{:S(2)}, u32[]{:S(2)}) collective-permute-start(bf16[8,10880]{1,0:T(8,128)(2,1)S(1)} %get-tuple-element.73), channel_id=1, source_target_pairs={{0,2},{1,3},{2,0},{3,1},{4,6},{5,7},{6,4},{7,5},{8,10},{9,11},{10,... | collective-permute-start | bytes 522248 | tf_op jit(solution)/shard_map/ppermute | solution.py:44
  5.9 1.5 %collective-permute-start.4 = (bf16[8,10880]{1,0:T(8,128)(2,1)S(1)}, bf16[8,10880]{1,0:T(8,128)(2,1)S(1)}, u32[]{:S(2)}, u32[]{:S(2)}) collective-permute-start(bf16[8,10880]{1,0:T(8,128)(2,1)S(1)} %get-tuple-element.74), channel_id=1, source_target_pairs={{0,4},{1,5},{2,6},{3,7},{4,0},{5,1},{6,2},{7,3},{8,12},{9,13},{10,... | collective-permute-start | bytes 522248 | tf_op jit(solution)/shard_map/ppermute | solution.py:44
  7.5 0.0 collective-permute-done.refs_3_
  7.5 1.5 %collective-permute-start.5 = (bf16[8,10880]{1,0:T(8,128)(2,1)S(1)}, bf16[8,10880]{1,0:T(8,128)(2,1)S(1)}, u32[]{:S(2)}, u32[]{:S(2)}) collective-permute-start(bf16[8,10880]{1,0:T(8,128)(2,1)S(1)} %get-tuple-element.75), channel_id=1, source_target_pairs={{0,6},{1,7},{2,4},{3,5},{4,2},{5,3},{6,0},{7,1},{8,14},{9,15},{10,... | collective-permute-start | bytes 522248 | tf_op jit(solution)/shard_map/ppermute | solution.py:44
  9.0 0.0 copy-start
  9.0 1.0 %copy-done = bf16[1,2,24,3584]{3,2,1,0:T(8,128)(2,1)S(1)} copy-done((bf16[1,2,24,3584]{3,2,1,0:T(8,128)(2,1)S(1)}, bf16[1,2,24,3584]{3,2,1,0:T(8,128)(2,1)}, u32[]{:S(2)}) %copy-start) | copy-done | bytes 344088
  10.0 0.3 shard_map.124
  10.3 0.0 collective-permute-done.1.refs_4_
  10.3 0.0 collective-permute-done.2.refs_5_
  10.3 2.7 %shard_map.123 = (bf16[3584,512]{1,0:T(8,128)(2,1)S(1)}, bf16[256,3584]{1,0:T(8,128)(2,1)S(1)}, bf16[512,3584]{1,0:T(8,128)(2,1)S(1)}, bf16[3584,256]{1,0:T(8,128)(2,1)S(1)}) custom-call(bf16[3584,128]{1,0:T(8,128)(2,1)} %bitcast.15, bf16[3584,128]{1,0:T(8,128)(2,1)} %bitcast.17, bf16[128,3584]{1,0:T(8,128)(2,1)} %bitcast.19, ...), custom_call_target="tpu_custom_call" | custom-call | tf_op jit(solution)/shard_map/pallas_call | solution.py:22
  13.0 0.0 collective-permute-done.3.refs_1_
  13.0 3.1 %collective-permute-done.4.refs_2_ = bf16[8,10880]{1,0:T(8,128)(2,1)S(1)} collective-permute-done((bf16[8,10880]{1,0:T(8,128)(2,1)S(1)}, bf16[8,10880]{1,0:T(8,128)(2,1)S(1)}, u32[]{:S(2)}, u32[]{:S(2)}) %collective-permute-start.4) | collective-permute-done | bytes 174112 | tf_op jit(solution)/shard_map/ppermute | solution.py:44
  16.2 0.0 collective-permute-done.5.refs_3_
  16.2 0.0 copy-done.1
  16.2 2.6 %shard_map.125 = (bf16[8,7168]{1,0:T(8,128)(2,1)S(1)}, bf16[8,7168]{1,0:T(8,128)(2,1)S(1)}, bf16[8,7168]{1,0:T(8,128)(2,1)S(1)}, bf16[8,7168]{1,0:T(8,128)(2,1)S(1)}) custom-call(f32[1,3584]{1,0:T(1,128)S(1)} %copy-done.1, bf16[3584,512]{1,0:T(8,128)(2,1)S(1)} %get-tuple-element.68.cols_ref, bf16[256,3584]{1,0:T(8,128)(2,1)S(1)} %get-tuple-element.69.rows_ref, ...), custom_call_target="tpu_custom_call" | custom-call | tf_op jit(solution)/shard_map/pallas_call | solution.py:22
  18.8 1.3 %collective-permute-start.6 = (bf16[8,7168]{1,0:T(8,128)(2,1)S(1)}, bf16[8,7168]{1,0:T(8,128)(2,1)S(1)}, u32[]{:S(2)}, u32[]{:S(2)}) collective-permute-start(bf16[8,7168]{1,0:T(8,128)(2,1)S(1)} %get-tuple-element.77), channel_id=1, source_target_pairs={{0,2},{1,3},{2,0},{3,1},{4,6},{5,7},{6,4},{7,5},{8,10},{9,11},{10,... | collective-permute-start | bytes 344072 | tf_op jit(solution)/shard_map/ppermute | solution.py:44
  20.1 0.8 %collective-permute-start.7 = (bf16[8,7168]{1,0:T(8,128)(2,1)S(1)}, bf16[8,7168]{1,0:T(8,128)(2,1)S(1)}, u32[]{:S(2)}, u32[]{:S(2)}) collective-permute-start(bf16[8,7168]{1,0:T(8,128)(2,1)S(1)} %get-tuple-element.78), channel_id=1, source_target_pairs={{0,4},{1,5},{2,6},{3,7},{4,0},{5,1},{6,2},{7,3},{8,12},{9,13},{10,... | collective-permute-start | bytes 344072 | tf_op jit(solution)/shard_map/ppermute | solution.py:44
  20.9 1.4 %collective-permute-start.8 = (bf16[8,7168]{1,0:T(8,128)(2,1)S(1)}, bf16[8,7168]{1,0:T(8,128)(2,1)S(1)}, u32[]{:S(2)}, u32[]{:S(2)}) collective-permute-start(bf16[8,7168]{1,0:T(8,128)(2,1)S(1)} %get-tuple-element.79), channel_id=1, source_target_pairs={{0,6},{1,7},{2,4},{3,5},{4,2},{5,3},{6,0},{7,1},{8,14},{9,15},{10,... | collective-permute-start | bytes 344072 | tf_op jit(solution)/shard_map/ppermute | solution.py:44
  22.3 1.8 %collective-permute-done.6.refs_2_ = bf16[8,7168]{1,0:T(8,128)(2,1)S(1)} collective-permute-done((bf16[8,7168]{1,0:T(8,128)(2,1)S(1)}, bf16[8,7168]{1,0:T(8,128)(2,1)S(1)}, u32[]{:S(2)}, u32[]{:S(2)}) %collective-permute-start.6) | collective-permute-done | bytes 114720 | tf_op jit(solution)/shard_map/ppermute | solution.py:44
  24.1 2.8 %collective-permute-done.7.refs_3_ = bf16[8,7168]{1,0:T(8,128)(2,1)S(1)} collective-permute-done((bf16[8,7168]{1,0:T(8,128)(2,1)S(1)}, bf16[8,7168]{1,0:T(8,128)(2,1)S(1)}, u32[]{:S(2)}, u32[]{:S(2)}) %collective-permute-start.7) | collective-permute-done | bytes 114720 | tf_op jit(solution)/shard_map/ppermute | solution.py:44
  27.0 0.0 collective-permute-done.8.refs_4_
  27.0 0.9 %shard_map.126 = (bf16[24,3584]{1,0:T(8,128)(2,1)S(1)}, bf16[24,3584]{1,0:T(8,128)(2,1)S(1)}) custom-call(f32[8,128]{1,0:T(8,128)S(1)} %get-tuple-element.52.refs_0_, bf16[8,7168]{1,0:T(8,128)(2,1)S(1)} %get-tuple-element.76.refs_1_, bf16[8,7168]{1,0:T(8,128)(2,1)S(1)} %collective-permute-done.6.refs_2_, bf16[8,7168]{1,0:T(8,128)(2,1)S(1)} %collective-permute-done.7.refs_3_, ...), custom_call_target="tpu_custom_call" | custom-call | tf_op jit(solution)/shard_map/pallas_call | solution.py:22
  27.9 1.6 %collective-permute-start.9 = (bf16[24,3584]{1,0:T(8,128)(2,1)S(1)}, bf16[24,3584]{1,0:T(8,128)(2,1)S(1)}, u32[]{:S(2)}, u32[]{:S(2)}) collective-permute-start(bf16[24,3584]{1,0:T(8,128)(2,1)S(1)} %get-tuple-element.86), channel_id=1, source_target_pairs={{0,8},{1,9},{2,10},{3,11},{4,12},{5,13},{6,14},{7,15},{8,0},{9,1},... | collective-permute-start | bytes 516104 | tf_op jit(solution)/shard_map/ppermute | solution.py:55
  29.5 1.2 %collective-permute-start.10 = (bf16[24,3584]{1,0:T(8,128)(2,1)S(1)}, bf16[24,3584]{1,0:T(8,128)(2,1)S(1)}, u32[]{:S(2)}, u32[]{:S(2)}) collective-permute-start(bf16[24,3584]{1,0:T(8,128)(2,1)S(1)} %get-tuple-element.87), channel_id=1, source_target_pairs={{0,2},{1,3},{2,0},{3,1},{4,6},{5,7},{6,4},{7,5},{8,16},{9,17},{10,... | collective-permute-start | bytes 516104 | tf_op jit(solution)/shard_map/ppermute | solution.py:55
  30.7 2.7 %collective-permute-done.9.refs_1_ = bf16[24,3584]{1,0:T(8,128)(2,1)S(1)} collective-permute-done((bf16[24,3584]{1,0:T(8,128)(2,1)S(1)}, bf16[24,3584]{1,0:T(8,128)(2,1)S(1)}, u32[]{:S(2)}, u32[]{:S(2)}) %collective-permute-start.9) | collective-permute-done | bytes 172064 | tf_op jit(solution)/shard_map/ppermute | solution.py:55
  33.4 1.6 %collective-permute-done.10.refs_2_ = bf16[24,3584]{1,0:T(8,128)(2,1)S(1)} collective-permute-done((bf16[24,3584]{1,0:T(8,128)(2,1)S(1)}, bf16[24,3584]{1,0:T(8,128)(2,1)S(1)}, u32[]{:S(2)}, u32[]{:S(2)}) %collective-permute-start.10) | collective-permute-done | bytes 172064 | tf_op jit(solution)/shard_map/ppermute | solution.py:55
  34.9 0.5 shard_map.127
  35.5 1.2 %collective-permute-start.11 = (bf16[8,7296]{1,0:T(8,128)(2,1)S(1)}, bf16[8,7296]{1,0:T(8,128)(2,1)S(1)}, u32[]{:S(2)}, u32[]{:S(2)}) collective-permute-start(bf16[8,7296]{1,0:T(8,128)(2,1)S(1)} %get-tuple-element.89), channel_id=1, source_target_pairs={{0,2},{1,3},{2,0},{3,1},{4,6},{5,7},{6,4},{7,5},{8,10},{9,11},{10,... | collective-permute-start | bytes 350216 | tf_op jit(solution)/shard_map/ppermute | solution.py:44
  36.7 1.1 %collective-permute-start.12 = (bf16[8,7296]{1,0:T(8,128)(2,1)S(1)}, bf16[8,7296]{1,0:T(8,128)(2,1)S(1)}, u32[]{:S(2)}, u32[]{:S(2)}) collective-permute-start(bf16[8,7296]{1,0:T(8,128)(2,1)S(1)} %get-tuple-element.90), channel_id=1, source_target_pairs={{0,4},{1,5},{2,6},{3,7},{4,0},{5,1},{6,2},{7,3},{8,12},{9,13},{10,... | collective-permute-start | bytes 350216 | tf_op jit(solution)/shard_map/ppermute | solution.py:44
  37.9 1.2 %collective-permute-start.13 = (bf16[8,7296]{1,0:T(8,128)(2,1)S(1)}, bf16[8,7296]{1,0:T(8,128)(2,1)S(1)}, u32[]{:S(2)}, u32[]{:S(2)}) collective-permute-start(bf16[8,7296]{1,0:T(8,128)(2,1)S(1)} %get-tuple-element.91), channel_id=1, source_target_pairs={{0,6},{1,7},{2,4},{3,5},{4,2},{5,3},{6,0},{7,1},{8,14},{9,15},{10,... | collective-permute-start | bytes 350216 | tf_op jit(solution)/shard_map/ppermute | solution.py:44
  39.0 1.2 %collective-permute-start.14 = (bf16[8,3584]{1,0:T(8,128)(2,1)S(1)}, bf16[8,3584]{1,0:T(8,128)(2,1)S(1)}, u32[]{:S(2)}, u32[]{:S(2)}) collective-permute-start(bf16[8,3584]{1,0:T(8,128)(2,1)S(1)} %get-tuple-element.93), channel_id=1, source_target_pairs={{0,2},{1,3},{2,0},{3,1},{4,6},{5,7},{6,4},{7,5},{8,10},{9,11},{10,... | collective-permute-start | bytes 172040 | tf_op jit(solution)/shard_map/ppermute | solution.py:44
  40.2 1.1 %collective-permute-start.15 = (bf16[8,3584]{1,0:T(8,128)(2,1)S(1)}, bf16[8,3584]{1,0:T(8,128)(2,1)S(1)}, u32[]{:S(2)}, u32[]{:S(2)}) collective-permute-start(bf16[8,3584]{1,0:T(8,128)(2,1)S(1)} %get-tuple-element.94), channel_id=1, source_target_pairs={{0,4},{1,5},{2,6},{3,7},{4,0},{5,1},{6,2},{7,3},{8,12},{9,13},{10,... | collective-permute-start | bytes 172040 | tf_op jit(solution)/shard_map/ppermute | solution.py:44
  41.3 2.9 %collective-permute-done.14.refs_5_ = bf16[8,3584]{1,0:T(8,128)(2,1)S(1)} collective-permute-done((bf16[8,3584]{1,0:T(8,128)(2,1)S(1)}, bf16[8,3584]{1,0:T(8,128)(2,1)S(1)}, u32[]{:S(2)}, u32[]{:S(2)}) %collective-permute-start.14) | collective-permute-done | bytes 57376 | tf_op jit(solution)/shard_map/ppermute | solution.py:44
  44.2 1.5 %collective-permute-start.16 = (bf16[8,3584]{1,0:T(8,128)(2,1)S(1)}, bf16[8,3584]{1,0:T(8,128)(2,1)S(1)}, u32[]{:S(2)}, u32[]{:S(2)}) collective-permute-start(bf16[8,3584]{1,0:T(8,128)(2,1)S(1)} %get-tuple-element.95), channel_id=1, source_target_pairs={{0,6},{1,7},{2,4},{3,5},{4,2},{5,3},{6,0},{7,1},{8,14},{9,15},{10,... | collective-permute-start | bytes 172040 | tf_op jit(solution)/shard_map/ppermute | solution.py:44
  45.7 0.0 collective-permute-done.15.refs_6_
  45.7 3.6 %collective-permute-done.16.refs_7_ = bf16[8,3584]{1,0:T(8,128)(2,1)S(1)} collective-permute-done((bf16[8,3584]{1,0:T(8,128)(2,1)S(1)}, bf16[8,3584]{1,0:T(8,128)(2,1)S(1)}, u32[]{:S(2)}, u32[]{:S(2)}) %collective-permute-start.16) | collective-permute-done | bytes 57376 | tf_op jit(solution)/shard_map/ppermute | solution.py:44
  49.3 0.0 collective-permute-done.11.refs_1_
  49.3 0.0 collective-permute-done.12.refs_2_
  49.3 0.0 collective-permute-done.13.refs_3_
  49.3 2.6 %shard_map.128 = (bf16[8,7168]{1,0:T(8,128)(2,1)S(1)}, bf16[8,7168]{1,0:T(8,128)(2,1)S(1)}, bf16[8,7168]{1,0:T(8,128)(2,1)S(1)}, bf16[8,7168]{1,0:T(8,128)(2,1)S(1)}) custom-call(f32[1,3584]{1,0:T(1,128)S(1)} %copy-done.1, bf16[3584,512]{1,0:T(8,128)(2,1)S(1)} %get-tuple-element.68.cols_ref, bf16[256,3584]{1,0:T(8,128)(2,1)S(1)} %get-tuple-element.69.rows_ref, ...), custom_call_target="tpu_custom_call" | custom-call | tf_op jit(solution)/shard_map/pallas_call | solution.py:22
  52.0 0.9 %collective-permute-start.17 = (bf16[8,7168]{1,0:T(8,128)(2,1)S(1)}, bf16[8,7168]{1,0:T(8,128)(2,1)S(1)}, u32[]{:S(2)}, u32[]{:S(2)}) collective-permute-start(bf16[8,7168]{1,0:T(8,128)(2,1)S(1)} %get-tuple-element.97), channel_id=1, source_target_pairs={{0,2},{1,3},{2,0},{3,1},{4,6},{5,7},{6,4},{7,5},{8,10},{9,11},{10,... | collective-permute-start | bytes 344072 | tf_op jit(solution)/shard_map/ppermute | solution.py:44
  52.9 1.2 %collective-permute-start.18 = (bf16[8,7168]{1,0:T(8,128)(2,1)S(1)}, bf16[8,7168]{1,0:T(8,128)(2,1)S(1)}, u32[]{:S(2)}, u32[]{:S(2)}) collective-permute-start(bf16[8,7168]{1,0:T(8,128)(2,1)S(1)} %get-tuple-element.98), channel_id=1, source_target_pairs={{0,4},{1,5},{2,6},{3,7},{4,0},{5,1},{6,2},{7,3},{8,12},{9,13},{10,... | collective-permute-start | bytes 344072 | tf_op jit(solution)/shard_map/ppermute | solution.py:44
  54.1 1.4 %collective-permute-start.19 = (bf16[8,7168]{1,0:T(8,128)(2,1)S(1)}, bf16[8,7168]{1,0:T(8,128)(2,1)S(1)}, u32[]{:S(2)}, u32[]{:S(2)}) collective-permute-start(bf16[8,7168]{1,0:T(8,128)(2,1)S(1)} %get-tuple-element.99), channel_id=1, source_target_pairs={{0,6},{1,7},{2,4},{3,5},{4,2},{5,3},{6,0},{7,1},{8,14},{9,15},{10,... | collective-permute-start | bytes 344072 | tf_op jit(solution)/shard_map/ppermute | solution.py:44
  55.5 1.3 %collective-permute-done.17.refs_2_ = bf16[8,7168]{1,0:T(8,128)(2,1)S(1)} collective-permute-done((bf16[8,7168]{1,0:T(8,128)(2,1)S(1)}, bf16[8,7168]{1,0:T(8,128)(2,1)S(1)}, u32[]{:S(2)}, u32[]{:S(2)}) %collective-permute-start.17) | collective-permute-done | bytes 114720 | tf_op jit(solution)/shard_map/ppermute | solution.py:44
  56.8 0.9 %collective-permute-done.18.refs_3_ = bf16[8,7168]{1,0:T(8,128)(2,1)S(1)} collective-permute-done((bf16[8,7168]{1,0:T(8,128)(2,1)S(1)}, bf16[8,7168]{1,0:T(8,128)(2,1)S(1)}, u32[]{:S(2)}, u32[]{:S(2)}) %collective-permute-start.18) | collective-permute-done | bytes 114720 | tf_op jit(solution)/shard_map/ppermute | solution.py:44
  57.7 2.1 %collective-permute-done.19.refs_4_ = bf16[8,7168]{1,0:T(8,128)(2,1)S(1)} collective-permute-done((bf16[8,7168]{1,0:T(8,128)(2,1)S(1)}, bf16[8,7168]{1,0:T(8,128)(2,1)S(1)}, u32[]{:S(2)}, u32[]{:S(2)}) %collective-permute-start.19) | collective-permute-done | bytes 114720 | tf_op jit(solution)/shard_map/ppermute | solution.py:44
  59.8 1.3 %shard_map.129 = (bf16[24,3584]{1,0:T(8,128)(2,1)}, bf16[24,3584]{1,0:T(8,128)(2,1)}) custom-call(f32[8,128]{1,0:T(8,128)S(1)} %get-tuple-element.52.refs_0_, bf16[8,7168]{1,0:T(8,128)(2,1)S(1)} %get-tuple-element.96.refs_1_, bf16[8,7168]{1,0:T(8,128)(2,1)S(1)} %collective-permute-done.17.refs_2_, bf16[8,7168]{1,0:T(8,128)(2,1)S(1)} %collective-permute-done.18.refs_3_, ...), custom_call_target="tpu_custom_call" | custom-call | tf_op jit(solution)/shard_map/pallas_call | solution.py:22
Async XLA Ops:
  0.6 15.5 %copy-start.1 = (f32[1,3584]{1,0:T(1,128)S(1)}, f32[1,3584]{1,0:T(1,128)}, u32[]{:S(2)}) copy-start(f32[1,3584]{1,0:T(1,128)} %gain_ref.3) | copy-start | bytes 43012
  2.3 5.1 %collective-permute-start = (bf16[3584,128]{1,0:T(8,128)(2,1)}, bf16[3584,128]{1,0:T(8,128)(2,1)S(1)}, u32[]{:S(2)}, u32[]{:S(2)}) collective-permute-start(bf16[3584,128]{1,0:T(8,128)(2,1)} %bitcast.14), channel_id=1, source_target_pairs={{0,1},{1,0},{2,3},{3,2},{4,5},{5,4},{6,7},{7,6},{8,9},{9,8},{10,11... | collective-permute-start | bytes 2752520 | tf_op jit(solution)/shard_map/ppermute | solution.py:37
  2.9 7.4 %collective-permute-start.1 = (bf16[3584,128]{1,0:T(8,128)(2,1)}, bf16[3584,128]{1,0:T(8,128)(2,1)S(1)}, u32[]{:S(2)}, u32[]{:S(2)}) collective-permute-start(bf16[3584,128]{1,0:T(8,128)(2,1)} %bitcast.16), channel_id=1, source_target_pairs={{0,1},{1,0},{2,3},{3,2},{4,5},{5,4},{6,7},{7,6},{8,9},{9,8},{10,11... | collective-permute-start | bytes 2752520 | tf_op jit(solution)/shard_map/ppermute | solution.py:37
  3.0 7.4 %collective-permute-start.2 = (bf16[128,3584]{1,0:T(8,128)(2,1)}, bf16[128,3584]{1,0:T(8,128)(2,1)S(1)}, u32[]{:S(2)}, u32[]{:S(2)}) collective-permute-start(bf16[128,3584]{1,0:T(8,128)(2,1)} %bitcast.18), channel_id=1, source_target_pairs={{0,1},{1,0},{2,3},{3,2},{4,5},{5,4},{6,7},{7,6},{8,9},{9,8},{10,11... | collective-permute-start | bytes 2752520 | tf_op jit(solution)/shard_map/ppermute | solution.py:37
  3.4 9.6 %collective-permute-start.3 = (bf16[8,10880]{1,0:T(8,128)(2,1)S(1)}, bf16[8,10880]{1,0:T(8,128)(2,1)S(1)}, u32[]{:S(2)}, u32[]{:S(2)}) collective-permute-start(bf16[8,10880]{1,0:T(8,128)(2,1)S(1)} %get-tuple-element.73), channel_id=1, source_target_pairs={{0,2},{1,3},{2,0},{3,1},{4,6},{5,7},{6,4},{7,5},{8,10},{9,11},{10,... | collective-permute-start | bytes 522248 | tf_op jit(solution)/shard_map/ppermute | solution.py:44
  5.9 10.2 %collective-permute-start.4 = (bf16[8,10880]{1,0:T(8,128)(2,1)S(1)}, bf16[8,10880]{1,0:T(8,128)(2,1)S(1)}, u32[]{:S(2)}, u32[]{:S(2)}) collective-permute-start(bf16[8,10880]{1,0:T(8,128)(2,1)S(1)} %get-tuple-element.74), channel_id=1, source_target_pairs={{0,4},{1,5},{2,6},{3,7},{4,0},{5,1},{6,2},{7,3},{8,12},{9,13},{10,... | collective-permute-start | bytes 522248 | tf_op jit(solution)/shard_map/ppermute | solution.py:44
  7.5 8.7 %collective-permute-start.5 = (bf16[8,10880]{1,0:T(8,128)(2,1)S(1)}, bf16[8,10880]{1,0:T(8,128)(2,1)S(1)}, u32[]{:S(2)}, u32[]{:S(2)}) collective-permute-start(bf16[8,10880]{1,0:T(8,128)(2,1)S(1)} %get-tuple-element.75), channel_id=1, source_target_pairs={{0,6},{1,7},{2,4},{3,5},{4,2},{5,3},{6,0},{7,1},{8,14},{9,15},{10,... | collective-permute-start | bytes 522248 | tf_op jit(solution)/shard_map/ppermute | solution.py:44
  9.0 1.0 %copy-start = (bf16[1,2,24,3584]{3,2,1,0:T(8,128)(2,1)S(1)}, bf16[1,2,24,3584]{3,2,1,0:T(8,128)(2,1)}, u32[]{:S(2)}) copy-start(bf16[1,2,24,3584]{3,2,1,0:T(8,128)(2,1)} %param.13) | copy-start | bytes 1032196
  18.8 5.4 %collective-permute-start.6 = (bf16[8,7168]{1,0:T(8,128)(2,1)S(1)}, bf16[8,7168]{1,0:T(8,128)(2,1)S(1)}, u32[]{:S(2)}, u32[]{:S(2)}) collective-permute-start(bf16[8,7168]{1,0:T(8,128)(2,1)S(1)} %get-tuple-element.77), channel_id=1, source_target_pairs={{0,2},{1,3},{2,0},{3,1},{4,6},{5,7},{6,4},{7,5},{8,10},{9,11},{10,... | collective-permute-start | bytes 344072 | tf_op jit(solution)/shard_map/ppermute | solution.py:44
  20.1 6.9 %collective-permute-start.7 = (bf16[8,7168]{1,0:T(8,128)(2,1)S(1)}, bf16[8,7168]{1,0:T(8,128)(2,1)S(1)}, u32[]{:S(2)}, u32[]{:S(2)}) collective-permute-start(bf16[8,7168]{1,0:T(8,128)(2,1)S(1)} %get-tuple-element.78), channel_id=1, source_target_pairs={{0,4},{1,5},{2,6},{3,7},{4,0},{5,1},{6,2},{7,3},{8,12},{9,13},{10,... | collective-permute-start | bytes 344072 | tf_op jit(solution)/shard_map/ppermute | solution.py:44
  20.9 6.1 %collective-permute-start.8 = (bf16[8,7168]{1,0:T(8,128)(2,1)S(1)}, bf16[8,7168]{1,0:T(8,128)(2,1)S(1)}, u32[]{:S(2)}, u32[]{:S(2)}) collective-permute-start(bf16[8,7168]{1,0:T(8,128)(2,1)S(1)} %get-tuple-element.79), channel_id=1, source_target_pairs={{0,6},{1,7},{2,4},{3,5},{4,2},{5,3},{6,0},{7,1},{8,14},{9,15},{10,... | collective-permute-start | bytes 344072 | tf_op jit(solution)/shard_map/ppermute | solution.py:44
  27.9 5.5 %collective-permute-start.9 = (bf16[24,3584]{1,0:T(8,128)(2,1)S(1)}, bf16[24,3584]{1,0:T(8,128)(2,1)S(1)}, u32[]{:S(2)}, u32[]{:S(2)}) collective-permute-start(bf16[24,3584]{1,0:T(8,128)(2,1)S(1)} %get-tuple-element.86), channel_id=1, source_target_pairs={{0,8},{1,9},{2,10},{3,11},{4,12},{5,13},{6,14},{7,15},{8,0},{9,1},... | collective-permute-start | bytes 516104 | tf_op jit(solution)/shard_map/ppermute | solution.py:55
  29.5 5.4 %collective-permute-start.10 = (bf16[24,3584]{1,0:T(8,128)(2,1)S(1)}, bf16[24,3584]{1,0:T(8,128)(2,1)S(1)}, u32[]{:S(2)}, u32[]{:S(2)}) collective-permute-start(bf16[24,3584]{1,0:T(8,128)(2,1)S(1)} %get-tuple-element.87), channel_id=1, source_target_pairs={{0,2},{1,3},{2,0},{3,1},{4,6},{5,7},{6,4},{7,5},{8,16},{9,17},{10,... | collective-permute-start | bytes 516104 | tf_op jit(solution)/shard_map/ppermute | solution.py:55
  35.5 13.8 %collective-permute-start.11 = (bf16[8,7296]{1,0:T(8,128)(2,1)S(1)}, bf16[8,7296]{1,0:T(8,128)(2,1)S(1)}, u32[]{:S(2)}, u32[]{:S(2)}) collective-permute-start(bf16[8,7296]{1,0:T(8,128)(2,1)S(1)} %get-tuple-element.89), channel_id=1, source_target_pairs={{0,2},{1,3},{2,0},{3,1},{4,6},{5,7},{6,4},{7,5},{8,10},{9,11},{10,... | collective-permute-start | bytes 350216 | tf_op jit(solution)/shard_map/ppermute | solution.py:44
  36.7 12.6 %collective-permute-start.12 = (bf16[8,7296]{1,0:T(8,128)(2,1)S(1)}, bf16[8,7296]{1,0:T(8,128)(2,1)S(1)}, u32[]{:S(2)}, u32[]{:S(2)}) collective-permute-start(bf16[8,7296]{1,0:T(8,128)(2,1)S(1)} %get-tuple-element.90), channel_id=1, source_target_pairs={{0,4},{1,5},{2,6},{3,7},{4,0},{5,1},{6,2},{7,3},{8,12},{9,13},{10,... | collective-permute-start | bytes 350216 | tf_op jit(solution)/shard_map/ppermute | solution.py:44
  37.9 11.5 %collective-permute-start.13 = (bf16[8,7296]{1,0:T(8,128)(2,1)S(1)}, bf16[8,7296]{1,0:T(8,128)(2,1)S(1)}, u32[]{:S(2)}, u32[]{:S(2)}) collective-permute-start(bf16[8,7296]{1,0:T(8,128)(2,1)S(1)} %get-tuple-element.91), channel_id=1, source_target_pairs={{0,6},{1,7},{2,4},{3,5},{4,2},{5,3},{6,0},{7,1},{8,14},{9,15},{10,... | collective-permute-start | bytes 350216 | tf_op jit(solution)/shard_map/ppermute | solution.py:44
  39.0 5.2 %collective-permute-start.14 = (bf16[8,3584]{1,0:T(8,128)(2,1)S(1)}, bf16[8,3584]{1,0:T(8,128)(2,1)S(1)}, u32[]{:S(2)}, u32[]{:S(2)}) collective-permute-start(bf16[8,3584]{1,0:T(8,128)(2,1)S(1)} %get-tuple-element.93), channel_id=1, source_target_pairs={{0,2},{1,3},{2,0},{3,1},{4,6},{5,7},{6,4},{7,5},{8,10},{9,11},{10,... | collective-permute-start | bytes 172040 | tf_op jit(solution)/shard_map/ppermute | solution.py:44
  40.2 5.5 %collective-permute-start.15 = (bf16[8,3584]{1,0:T(8,128)(2,1)S(1)}, bf16[8,3584]{1,0:T(8,128)(2,1)S(1)}, u32[]{:S(2)}, u32[]{:S(2)}) collective-permute-start(bf16[8,3584]{1,0:T(8,128)(2,1)S(1)} %get-tuple-element.94), channel_id=1, source_target_pairs={{0,4},{1,5},{2,6},{3,7},{4,0},{5,1},{6,2},{7,3},{8,12},{9,13},{10,... | collective-permute-start | bytes 172040 | tf_op jit(solution)/shard_map/ppermute | solution.py:44
  44.2 5.1 %collective-permute-start.16 = (bf16[8,3584]{1,0:T(8,128)(2,1)S(1)}, bf16[8,3584]{1,0:T(8,128)(2,1)S(1)}, u32[]{:S(2)}, u32[]{:S(2)}) collective-permute-start(bf16[8,3584]{1,0:T(8,128)(2,1)S(1)} %get-tuple-element.95), channel_id=1, source_target_pairs={{0,6},{1,7},{2,4},{3,5},{4,2},{5,3},{6,0},{7,1},{8,14},{9,15},{10,... | collective-permute-start | bytes 172040 | tf_op jit(solution)/shard_map/ppermute | solution.py:44
  52.0 4.9 %collective-permute-start.17 = (bf16[8,7168]{1,0:T(8,128)(2,1)S(1)}, bf16[8,7168]{1,0:T(8,128)(2,1)S(1)}, u32[]{:S(2)}, u32[]{:S(2)}) collective-permute-start(bf16[8,7168]{1,0:T(8,128)(2,1)S(1)} %get-tuple-element.97), channel_id=1, source_target_pairs={{0,2},{1,3},{2,0},{3,1},{4,6},{5,7},{6,4},{7,5},{8,10},{9,11},{10,... | collective-permute-start | bytes 344072 | tf_op jit(solution)/shard_map/ppermute | solution.py:44
  52.9 4.8 %collective-permute-start.18 = (bf16[8,7168]{1,0:T(8,128)(2,1)S(1)}, bf16[8,7168]{1,0:T(8,128)(2,1)S(1)}, u32[]{:S(2)}, u32[]{:S(2)}) collective-permute-start(bf16[8,7168]{1,0:T(8,128)(2,1)S(1)} %get-tuple-element.98), channel_id=1, source_target_pairs={{0,4},{1,5},{2,6},{3,7},{4,0},{5,1},{6,2},{7,3},{8,12},{9,13},{10,... | collective-permute-start | bytes 344072 | tf_op jit(solution)/shard_map/ppermute | solution.py:44
  54.1 5.7 %collective-permute-start.19 = (bf16[8,7168]{1,0:T(8,128)(2,1)S(1)}, bf16[8,7168]{1,0:T(8,128)(2,1)S(1)}, u32[]{:S(2)}, u32[]{:S(2)}) collective-permute-start(bf16[8,7168]{1,0:T(8,128)(2,1)S(1)} %get-tuple-element.99), channel_id=1, source_target_pairs={{0,6},{1,7},{2,4},{3,5},{4,2},{5,3},{6,0},{7,1},{8,14},{9,15},{10,... | collective-permute-start | bytes 344072 | tf_op jit(solution)/shard_map/ppermute | solution.py:44

commit v2 on v1

--- a/solution.py
+++ b/solution.py
@@ -55,33 +55,37 @@
     return lax.ppermute(array, ("pipe", "expert"), list(enumerate(target)))
 
 
-def slot_of(rows, line, tokens, axis):
+def slot_hits(routes):
+    count, tokens = routes.shape
     chip, _ = place()
-    row, col = rows[line : line + 1, :tokens], rows.T[:tokens, line : line + 1]
+    routes = routes.astype(jnp.int32)
+    expert = lax.broadcasted_iota(jnp.int32, (EXPERTS, tokens), 0)
+    named = [jnp.where(expert == routes[i : i + 1], 1.0, 0.0) for i in range(count)]
     down = lax.broadcasted_iota(jnp.int32, (tokens, tokens), 0)
     across = lax.broadcasted_iota(jnp.int32, (tokens, tokens), 1)
-    earlier = down < across if axis == 0 else across < down
-    rank = jnp.sum(jnp.where((row == col) & earlier, 1, 0), axis=axis, keepdims=True)
-    route = (row if axis == 0 else col).astype(jnp.int32)
-    return (route ^ chip) * SLOT + rank
-
-
-def table_to_slots(rows, line, tokens, wanted=True):
-    down = lax.broadcasted_iota(jnp.int32, (EXPERTS * SLOT, tokens), 0)
-    hit = (down == slot_of(rows, line, tokens, 0)) & wanted
-    return jnp.where(hit, 1.0, 0.0).astype(BF16)
-
-
-def table_to_tokens(rows, line, tokens):
-    across = lax.broadcasted_iota(jnp.int32, (tokens, EXPERTS * SLOT), 1)
-    return jnp.where(across == slot_of(rows, line, tokens, 1), 1.0, 0.0).astype(BF16)
-
-
-def gate_lanes(rows, line, tokens, lane):
-    gate = rows.T[:tokens, line : line + 1]
-    high = gate.astype(BF16).astype(F32)
-    at = lax.broadcasted_iota(jnp.int32, (tokens, LANES), 1) - lane
-    return jnp.where(at == 0, high, jnp.where(at == 1, gate - high, 0.0)).astype(BF16)
+    earlier = jnp.where(down < across, 1.0, 0.0).astype(BF16)
+    stacked = jnp.concatenate(named, axis=0)
+    before = placed(stacked.astype(BF16), earlier) * stacked
+    slot = lax.broadcasted_iota(jnp.int32, (EXPERTS * SLOT, tokens), 0)
+    hits = []
+    for i in range(count):
+        rank = jnp.sum(before[i * EXPERTS : (i + 1) * EXPERTS], axis=0, keepdims=True)
+        hits.append(slot == (routes[i : i + 1] ^ chip) * SLOT + rank.astype(jnp.int32))
+    return hits
+
+
+def as_table(hits):
+    return jnp.where(hits, 1.0, 0.0)
+
+
+def slot_gates(fwd_hits, bwd_hits, fwd_gates, bwd_gates):
+    lane = lax.broadcasted_iota(jnp.int32, (EXPERTS * SLOT, LANES), 1)
+    value = jnp.zeros(lane.shape, F32)
+    for i, (hits, gates) in enumerate(((fwd_hits, fwd_gates), (bwd_hits, bwd_gates))):
+        gate = jnp.sum(jnp.where(hits, gates, 0.0), axis=1, keepdims=True)
+        high = gate.astype(BF16).astype(F32)
+        value = jnp.where(lane == 2 * i, high, jnp.where(lane == 2 * i + 1, gate - high, value))
+    return value
 
 
 def placed(table, rows):
@@ -91,12 +95,6 @@
 def put_pieces(outs, at, value):
     for m, out in enumerate(outs):
         out[:, at : at + value.shape[1]] = value[m * SLOT : (m + 1) * SLOT].astype(BF16)
-
-
-def put_gates(rows, step, steps, tokens, fwd_table, bwd_table, outs):
-    value = placed(fwd_table, gate_lanes(rows, 2 * steps + step, tokens, 0))
-    value = value + placed(bwd_table, gate_lanes(rows, 3 * steps + step, tokens, 2))
-    put_pieces(outs, 0, value)
 
 
 def first_spread_body(steps, tokens, *refs):
@@ -114,13 +112,13 @@
     for i in range(4):
         copies[i].wait()
         lines[i * steps : (i + 1) * steps, :tokens] = scratch[i][...].astype(F32)
-    rows = lines[...]
-    fwd_table = table_to_slots(rows, 0, tokens)
-    bwd_table = table_to_slots(rows, steps, tokens)
-    put_gates(rows, 0, steps, tokens, fwd_table, bwd_table, outs)
-    for i, (table, at) in enumerate(((fwd_table, 0), (bwd_table, 1), (bwd_table, 2))):
+    routes = jnp.concatenate([scratch[0][0:1], scratch[1][0:1]], axis=0)
+    fwd_hits, bwd_hits = slot_hits(routes)
+    put_pieces(outs, 0, slot_gates(fwd_hits, bwd_hits, scratch[2][0:1], scratch[3][0:1]))
+    fwd_table, bwd_table = as_table(fwd_hits).astype(BF16), as_table(bwd_hits).astype(BF16)
+    for i, table in enumerate((fwd_table, bwd_table, bwd_table)):
         copies[4 + i].wait()
-        put_pieces(outs, LANES + at * width, placed(table, scratch[4 + i][...]))
+        put_pieces(outs, LANES + i * width, placed(table, scratch[4 + i][...]))
 
 
 def first_spread(small, state, grad, saved):
@@ -140,50 +138,71 @@
     )
 
 
-def spread_saved_body(step, steps, tokens, *refs):
-    lines, saved, outs = refs[0], refs[1], refs[2:]
-    table = table_to_slots(lines[...], steps + step, tokens)
-    put_pieces(outs, 0, placed(table, saved[step * tokens : (step + 1) * tokens, :]))
-
-
-def spread_body(step, steps, tokens, *refs):
-    lines, low, high, outs = refs[0], refs[1], refs[2], refs[3:]
+def prepare_body(steps, tokens, *refs):
+    lines, saved, to_tokens, to_slots, gates, later = *refs[:5], refs[5:]
+    rank, last = lax.axis_index("pipe"), lax.axis_size("pipe") - 1
+    rows = lines[...]
+    across = slice(0, tokens)
+    for step in range(steps):
+        at = (step, steps + step, 2 * steps + step, 3 * steps + step)
+        fwd_row, bwd_row, fwd_gate, bwd_gate = (rows[i : i + 1, across] for i in at)
+        hits = slot_hits(jnp.concatenate([fwd_row, bwd_row], axis=0))
+        gates[step] = slot_gates(*hits, fwd_gate, bwd_gate).astype(BF16)
+        for i, end in enumerate((0, last)):
+            table = as_table(hits[i])
+            to_tokens[2 * step + i] = table.T.astype(BF16)
+            come = as_table(hits[i] & (rank != end)).astype(BF16)
+            to_slots[2 * step + i] = come
+        if step:
+            table = table.astype(BF16)
+            outs = later[(step - 1) * EXPERTS : step * EXPERTS]
+            put_pieces(outs, 0, placed(table, saved[step * tokens : (step + 1) * tokens, :]))
+
+
+def prepare(lines, saved, steps, tokens):
+    slots = EXPERTS * SLOT
+    outs = [
+        jax.ShapeDtypeStruct((2 * steps, tokens, slots), BF16),
+        jax.ShapeDtypeStruct((2 * steps, slots, tokens), BF16),
+        jax.ShapeDtypeStruct((steps, slots, LANES), BF16),
+    ]
+    outs += [jax.ShapeDtypeStruct((SLOT, saved.shape[1]), BF16)] * (EXPERTS * (steps - 1))
+    body = functools.partial(prepare_body, steps, tokens)
+    to_tokens, to_slots, gates, *later = call(body, outs, [lines, saved])
+    later = [later[i * EXPERTS : (i + 1) * EXPERTS] for i in range(steps - 1)]
+    return (to_tokens, to_slots, gates), later
+
+
+def spread_body(step, tables, gates, low, high, *outs):
     width = low.shape[1]
-    rank, last = lax.axis_index("pipe"), lax.axis_size("pipe") - 1
-    even = rank % 2 == 0
-    rows = lines[...]
-    fwd_table = table_to_slots(rows, step, tokens, rank != 0)
-    bwd_table = table_to_slots(rows, steps + step, tokens, rank != last)
-    put_gates(rows, step, steps, tokens, fwd_table, bwd_table, outs)
+    even = lax.axis_index("pipe") % 2 == 0
+    for m, out in enumerate(outs):
+        out[:, :LANES] = gates[step, m * SLOT : (m + 1) * SLOT, :]
 
     def put(forward, backward):
-        put_pieces(outs, LANES, placed(fwd_table, forward[...]))
-        put_pieces(outs, LANES + width, placed(bwd_table, backward[...]))
+        put_pieces(outs, LANES, placed(tables[2 * step], forward[...]))
+        put_pieces(outs, LANES + width, placed(tables[2 * step + 1], backward[...]))
 
     pl.when(even)(lambda: put(high, low))
     pl.when(jnp.logical_not(even))(lambda: put(low, high))
 
 
-def gather_body(step, steps, tokens, last, *refs):
-    lines, pieces, outs = refs[0], refs[1 : 1 + EXPERTS], refs[1 + EXPERTS :]
+def gather_body(step, last, tables, *refs):
+    pieces, outs = refs[:EXPERTS], refs[EXPERTS:]
     width = outs[0].shape[1]
-    rows = lines[...]
-    even = lax.axis_index("pipe") % 2 == 0
-    for stream, line in enumerate((step, steps + step)):
-        lanes = slice(stream * width, (stream + 1) * width)
-        slots = jnp.concatenate([p[:, lanes] for p in pieces], axis=0)
-        value = placed(table_to_tokens(rows, line, tokens), slots).astype(BF16)
-        if last:
-            outs[stream][...] = value
-            continue
-
-        @pl.when(even)
-        def _():
-            outs[stream][...] = value
-
-        @pl.when(jnp.logical_not(even))
-        def _():
-            outs[1 - stream][...] = value
+
+    def put(*targets):
+        for stream, out in enumerate(targets):
+            lanes = slice(stream * width, (stream + 1) * width)
+            slots = jnp.concatenate([p[:, lanes] for p in pieces], axis=0)
+            out[...] = placed(tables[2 * step + stream], slots).astype(BF16)
+
+    if last:
+        put(*outs)
+    else:
+        even = lax.axis_index("pipe") % 2 == 0
+        pl.when(even)(lambda: put(outs[0], outs[1]))
+        pl.when(jnp.logical_not(even))(lambda: put(outs[1], outs[0]))
 
 
 def pack_body(*refs):
@@ -308,29 +327,26 @@
     made, own = lax.optimization_barrier((made, (w_gate[0], w_up[0], w_down[0])))
     pieces = exchange(made)
     weights = pack(own)
-    one = [jax.ShapeDtypeStruct((SLOT, width), BF16)] * EXPERTS
     two = [jax.ShapeDtypeStruct((SLOT, 2 * width), BF16)] * EXPERTS
     main = [jax.ShapeDtypeStruct((SLOT, LANES + 2 * width), BF16)] * EXPERTS
     state = [jax.ShapeDtypeStruct((tokens, width), BF16)] * 2
-    later = []
-    for step in range(1, steps):
-        body = functools.partial(spread_saved_body, step, steps, tokens)
-        later.append(call(body, one, [lines, saved]))
-    weights, later = lax.optimization_barrier((weights, later))
+    tables, later = prepare(lines, saved, steps, tokens)
+    weights, tables, later = lax.optimization_barrier((weights, tables, later))
+    to_tokens, to_slots, gates = tables
     for step in range(steps):
         back = call(expert_body, two, [norm_gain, *weights, *pieces])
         last = step + 1 == steps
         back = exchange(back)
-        body = functools.partial(gather_body, step, steps, tokens, last)
-        made = call(body, state, [lines, *back])
+        body = functools.partial(gather_body, step, last)
+        made = call(body, state, [to_tokens, *back])
         if last:
             return made[0][None], made[1][None]
         made, ahead = lax.optimization_barrier((made, later[step]))
         high = swap_ranks(made[1], 1)
         low = swap_ranks(made[0], 0)
         ahead = exchange(ahead)
-        body = functools.partial(spread_body, step + 1, steps, tokens)
-        made = call(body, main, [lines, low, high])
+        body = functools.partial(spread_body, step + 1)
+        made = call(body, main, [to_slots, gates, low, high])
         pieces = exchange(made) + ahead
 
 

time: 61.3 us -> 59.5 us (0.971)
  waiting for transfers between devices: 22.7 us -> 21.4 us
  Pallas kernels: 12.7 us -> 11.4 us
  starting transfers between devices: 23.9 us -> 24.8 us
    pallas_call x8, Pallas kernels: 12.7 us -> 11.4 us  [call(): pl.pallas_call(body, out_shape=outs, compiler_params=pltpu.CompilerParams...]
    ppermute x2, waiting for transfers between devices: 4.24 us -> 3.41 us  [swap_ranks(): return lax.ppermute(array, ('pipe', 'expert'), list(enumerate(target)))]
where the time goes in v2:
time: 59.5 us; the launch traced here: 59.3 us
  starting transfers between devices  24.8 us (42%)
  waiting for transfers between devices  21.4 us (36%)
  Pallas kernels  11.4 us (19%)
  local copies, waits for them, and re-layouts  0.98 us (2%)
  between operations  0.74 us (1%)
    ppermute x15, starting transfers between devices, exchange(): moved.append(lax.ppermute(pieces[m], 'expert', pairs))  20.6 us
    ppermute x15, waiting for transfers between devices, exchange(): moved.append(lax.ppermute(pieces[m], 'expert', pairs))  18 us
    pallas_call x8, Pallas kernels, call(): pl.pallas_call(body, out_shape=outs, compiler_params=pltpu.CompilerParams...  11.4 us
    ppermute x2, waiting for transfers between devices, swap_ranks(): return lax.ppermute(array, ('pipe', 'expert'), list(enumerate(target)))  3.41 us
    ppermute x2, starting transfers between devices, swap_ranks(): return lax.ppermute(array, ('pipe', 'expert'), list(enumerate(target)))  3.22 us
  transfers between devices with their start and end apart: 20, of which 10 were waited for; matrix products, arithmetic and copies ran while one was open for 0% of the time, Pallas kernels for 5%

profile of v2, /device:TPU:0, one launch (start us, length us, event | category | flops | bytes accessed | tf_op | source)
XLA Modules:
  0.0 59.3 jit_solution(8844375311098641174)
XLA Ops:
  0.6 0.0 copy-start.1
  0.6 1.6 %shard_map.122 = (f32[8,128]{1,0:T(8,128)S(1)}, bf16[8,10880]{1,0:T(8,128)(2,1)S(1)}, bf16[8,10880]{1,0:T(8,128)(2,1)S(1)}, bf16[8,10880]{1,0:T(8,128)(2,1)S(1)}, bf16[8,10880]{1,0:T(8,128)(2,1)S(1)}) custom-call(s32[2,24]{1,0:T(2,128)} %bitcast.22, s32[2,24]{1,0:T(2,128)} %bitcast.23, f32[2,24]{1,0:T(2,128)} %bitcast.24, f32[2,24]{1,0:T(2,128)} %bitcast.25, ...), custom_call_target="tpu_custom_call" | custom-call | tf_op jit(solution)/shard_map/pallas_call | solution.py:22
  2.3 0.6 collective-permute-start
  2.8 0.1 collective-permute-start.1
  2.9 0.4 collective-permute-start.2
  3.4 2.6 %collective-permute-start.3 = (bf16[8,10880]{1,0:T(8,128)(2,1)S(1)}, bf16[8,10880]{1,0:T(8,128)(2,1)S(1)}, u32[]{:S(2)}, u32[]{:S(2)}) collective-permute-start(bf16[8,10880]{1,0:T(8,128)(2,1)S(1)} %get-tuple-element.85), channel_id=1, source_target_pairs={{0,2},{1,3},{2,0},{3,1},{4,6},{5,7},{6,4},{7,5},{8,10},{9,11},{10,... | collective-permute-start | bytes 522248 | tf_op jit(solution)/shard_map/ppermute | solution.py:44
  5.9 1.5 %collective-permute-start.4 = (bf16[8,10880]{1,0:T(8,128)(2,1)S(1)}, bf16[8,10880]{1,0:T(8,128)(2,1)S(1)}, u32[]{:S(2)}, u32[]{:S(2)}) collective-permute-start(bf16[8,10880]{1,0:T(8,128)(2,1)S(1)} %get-tuple-element.86), channel_id=1, source_target_pairs={{0,4},{1,5},{2,6},{3,7},{4,0},{5,1},{6,2},{7,3},{8,12},{9,13},{10,... | collective-permute-start | bytes 522248 | tf_op jit(solution)/shard_map/ppermute | solution.py:44
  7.4 0.0 collective-permute-done.refs_3_
  7.4 1.5 %collective-permute-start.5 = (bf16[8,10880]{1,0:T(8,128)(2,1)S(1)}, bf16[8,10880]{1,0:T(8,128)(2,1)S(1)}, u32[]{:S(2)}, u32[]{:S(2)}) collective-permute-start(bf16[8,10880]{1,0:T(8,128)(2,1)S(1)} %get-tuple-element.87), channel_id=1, source_target_pairs={{0,6},{1,7},{2,4},{3,5},{4,2},{5,3},{6,0},{7,1},{8,14},{9,15},{10,... | collective-permute-start | bytes 522248 | tf_op jit(solution)/shard_map/ppermute | solution.py:44
  9.0 0.0 copy-start
  9.0 1.0 %copy-done = bf16[1,2,24,3584]{3,2,1,0:T(8,128)(2,1)S(1)} copy-done((bf16[1,2,24,3584]{3,2,1,0:T(8,128)(2,1)S(1)}, bf16[1,2,24,3584]{3,2,1,0:T(8,128)(2,1)}, u32[]{:S(2)}) %copy-start) | copy-done | bytes 344088
  9.9 0.3 shard_map.124
  10.3 0.0 collective-permute-done.1.refs_4_
  10.3 0.0 collective-permute-done.2.refs_5_
  10.3 2.7 %shard_map.123 = (bf16[3584,512]{1,0:T(8,128)(2,1)S(1)}, bf16[256,3584]{1,0:T(8,128)(2,1)S(1)}, bf16[512,3584]{1,0:T(8,128)(2,1)S(1)}, bf16[3584,256]{1,0:T(8,128)(2,1)S(1)}) custom-call(bf16[3584,128]{1,0:T(8,128)(2,1)} %bitcast.15, bf16[3584,128]{1,0:T(8,128)(2,1)} %bitcast.17, bf16[128,3584]{1,0:T(8,128)(2,1)} %bitcast.19, ...), custom_call_target="tpu_custom_call" | custom-call | tf_op jit(solution)/shard_map/pallas_call | solution.py:22
  13.0 0.0 collective-permute-done.3.refs_1_
  13.0 3.1 %collective-permute-done.4.refs_2_ = bf16[8,10880]{1,0:T(8,128)(2,1)S(1)} collective-permute-done((bf16[8,10880]{1,0:T(8,128)(2,1)S(1)}, bf16[8,10880]{1,0:T(8,128)(2,1)S(1)}, u32[]{:S(2)}, u32[]{:S(2)}) %collective-permute-start.4) | collective-permute-done | bytes 174112 | tf_op jit(solution)/shard_map/ppermute | solution.py:44
  16.1 0.0 collective-permute-done.5.refs_3_
  16.1 0.0 copy-done.1
  16.1 2.6 %shard_map.125 = (bf16[8,7168]{1,0:T(8,128)(2,1)S(1)}, bf16[8,7168]{1,0:T(8,128)(2,1)S(1)}, bf16[8,7168]{1,0:T(8,128)(2,1)S(1)}, bf16[8,7168]{1,0:T(8,128)(2,1)S(1)}) custom-call(f32[1,3584]{1,0:T(1,128)S(1)} %copy-done.1, bf16[3584,512]{1,0:T(8,128)(2,1)S(1)} %get-tuple-element.78.cols_ref, bf16[256,3584]{1,0:T(8,128)(2,1)S(1)} %get-tuple-element.79.rows_ref, ...), custom_call_target="tpu_custom_call" | custom-call | tf_op jit(solution)/shard_map/pallas_call | solution.py:22
  18.8 1.3 %collective-permute-start.6 = (bf16[8,7168]{1,0:T(8,128)(2,1)S(1)}, bf16[8,7168]{1,0:T(8,128)(2,1)S(1)}, u32[]{:S(2)}, u32[]{:S(2)}) collective-permute-start(bf16[8,7168]{1,0:T(8,128)(2,1)S(1)} %get-tuple-element.89), channel_id=1, source_target_pairs={{0,2},{1,3},{2,0},{3,1},{4,6},{5,7},{6,4},{7,5},{8,10},{9,11},{10,... | collective-permute-start | bytes 344072 | tf_op jit(solution)/shard_map/ppermute | solution.py:44
  20.1 0.8 %collective-permute-start.7 = (bf16[8,7168]{1,0:T(8,128)(2,1)S(1)}, bf16[8,7168]{1,0:T(8,128)(2,1)S(1)}, u32[]{:S(2)}, u32[]{:S(2)}) collective-permute-start(bf16[8,7168]{1,0:T(8,128)(2,1)S(1)} %get-tuple-element.90), channel_id=1, source_target_pairs={{0,4},{1,5},{2,6},{3,7},{4,0},{5,1},{6,2},{7,3},{8,12},{9,13},{10,... | collective-permute-start | bytes 344072 | tf_op jit(solution)/shard_map/ppermute | solution.py:44
  20.9 1.4 %collective-permute-start.8 = (bf16[8,7168]{1,0:T(8,128)(2,1)S(1)}, bf16[8,7168]{1,0:T(8,128)(2,1)S(1)}, u32[]{:S(2)}, u32[]{:S(2)}) collective-permute-start(bf16[8,7168]{1,0:T(8,128)(2,1)S(1)} %get-tuple-element.91), channel_id=1, source_target_pairs={{0,6},{1,7},{2,4},{3,5},{4,2},{5,3},{6,0},{7,1},{8,14},{9,15},{10,... | collective-permute-start | bytes 344072 | tf_op jit(solution)/shard_map/ppermute | solution.py:44
  22.3 1.8 %collective-permute-done.6.refs_1_ = bf16[8,7168]{1,0:T(8,128)(2,1)S(1)} collective-permute-done((bf16[8,7168]{1,0:T(8,128)(2,1)S(1)}, bf16[8,7168]{1,0:T(8,128)(2,1)S(1)}, u32[]{:S(2)}, u32[]{:S(2)}) %collective-permute-start.6) | collective-permute-done | bytes 114720 | tf_op jit(solution)/shard_map/ppermute | solution.py:44
  24.1 2.8 %collective-permute-done.7.refs_2_ = bf16[8,7168]{1,0:T(8,128)(2,1)S(1)} collective-permute-done((bf16[8,7168]{1,0:T(8,128)(2,1)S(1)}, bf16[8,7168]{1,0:T(8,128)(2,1)S(1)}, u32[]{:S(2)}, u32[]{:S(2)}) %collective-permute-start.7) | collective-permute-done | bytes 114720 | tf_op jit(solution)/shard_map/ppermute | solution.py:44
  26.9 0.0 collective-permute-done.8.refs_3_
  26.9 0.3 shard_map.126
  27.2 1.2 %collective-permute-start.10 = (bf16[24,3584]{1,0:T(8,128)(2,1)S(1)}, bf16[24,3584]{1,0:T(8,128)(2,1)S(1)}, u32[]{:S(2)}, u32[]{:S(2)}) collective-permute-start(bf16[24,3584]{1,0:T(8,128)(2,1)S(1)} %get-tuple-element.99), channel_id=1, source_target_pairs={{0,2},{1,3},{2,0},{3,1},{4,6},{5,7},{6,4},{7,5},{8,16},{9,17},{10,... | collective-permute-start | bytes 516104 | tf_op jit(solution)/shard_map/ppermute | solution.py:55
  28.4 2.0 %collective-permute-start.9 = (bf16[24,3584]{1,0:T(8,128)(2,1)S(1)}, bf16[24,3584]{1,0:T(8,128)(2,1)S(1)}, u32[]{:S(2)}, u32[]{:S(2)}) collective-permute-start(bf16[24,3584]{1,0:T(8,128)(2,1)S(1)} %get-tuple-element.98), channel_id=1, source_target_pairs={{0,8},{1,9},{2,10},{3,11},{4,12},{5,13},{6,14},{7,15},{8,0},{9,1},... | collective-permute-start | bytes 516104 | tf_op jit(solution)/shard_map/ppermute | solution.py:55
  30.4 2.3 %collective-permute-done.10.high = bf16[24,3584]{1,0:T(8,128)(2,1)S(1)} collective-permute-done((bf16[24,3584]{1,0:T(8,128)(2,1)S(1)}, bf16[24,3584]{1,0:T(8,128)(2,1)S(1)}, u32[]{:S(2)}, u32[]{:S(2)}) %collective-permute-start.10) | collective-permute-done | bytes 172064 | tf_op jit(solution)/shard_map/ppermute | solution.py:55
  32.7 1.2 %collective-permute-done.9.low = bf16[24,3584]{1,0:T(8,128)(2,1)S(1)} collective-permute-done((bf16[24,3584]{1,0:T(8,128)(2,1)S(1)}, bf16[24,3584]{1,0:T(8,128)(2,1)S(1)}, u32[]{:S(2)}, u32[]{:S(2)}) %collective-permute-start.9) | collective-permute-done | bytes 172064 | tf_op jit(solution)/shard_map/ppermute | solution.py:55
  33.8 0.3 shard_map.127
  34.1 1.2 %collective-permute-start.11 = (bf16[8,7296]{1,0:T(8,128)(2,1)S(1)}, bf16[8,7296]{1,0:T(8,128)(2,1)S(1)}, u32[]{:S(2)}, u32[]{:S(2)}) collective-permute-start(bf16[8,7296]{1,0:T(8,128)(2,1)S(1)} %get-tuple-element.101), channel_id=1, source_target_pairs={{0,2},{1,3},{2,0},{3,1},{4,6},{5,7},{6,4},{7,5},{8,10},{9,11},{10,... | collective-permute-start | bytes 350216 | tf_op jit(solution)/shard_map/ppermute | solution.py:44
  35.3 1.1 %collective-permute-start.12 = (bf16[8,7296]{1,0:T(8,128)(2,1)S(1)}, bf16[8,7296]{1,0:T(8,128)(2,1)S(1)}, u32[]{:S(2)}, u32[]{:S(2)}) collective-permute-start(bf16[8,7296]{1,0:T(8,128)(2,1)S(1)} %get-tuple-element.102), channel_id=1, source_target_pairs={{0,4},{1,5},{2,6},{3,7},{4,0},{5,1},{6,2},{7,3},{8,12},{9,13},{10,... | collective-permute-start | bytes 350216 | tf_op jit(solution)/shard_map/ppermute | solution.py:44
  36.4 1.2 %collective-permute-start.13 = (bf16[8,7296]{1,0:T(8,128)(2,1)S(1)}, bf16[8,7296]{1,0:T(8,128)(2,1)S(1)}, u32[]{:S(2)}, u32[]{:S(2)}) collective-permute-start(bf16[8,7296]{1,0:T(8,128)(2,1)S(1)} %get-tuple-element.103), channel_id=1, source_target_pairs={{0,6},{1,7},{2,4},{3,5},{4,2},{5,3},{6,0},{7,1},{8,14},{9,15},{10,... | collective-permute-start | bytes 350216 | tf_op jit(solution)/shard_map/ppermute | solution.py:44
  37.7 1.1 %collective-permute-start.14 = (bf16[8,3584]{1,0:T(8,128)(2,1)S(1)}, bf16[8,3584]{1,0:T(8,128)(2,1)S(1)}, u32[]{:S(2)}, u32[]{:S(2)}) collective-permute-start(bf16[8,3584]{1,0:T(8,128)(2,1)S(1)} %get-tuple-element.105), channel_id=1, source_target_pairs={{0,2},{1,3},{2,0},{3,1},{4,6},{5,7},{6,4},{7,5},{8,10},{9,11},{10,... | collective-permute-start | bytes 172040 | tf_op jit(solution)/shard_map/ppermute | solution.py:44
  38.8 1.1 %collective-permute-start.15 = (bf16[8,3584]{1,0:T(8,128)(2,1)S(1)}, bf16[8,3584]{1,0:T(8,128)(2,1)S(1)}, u32[]{:S(2)}, u32[]{:S(2)}) collective-permute-start(bf16[8,3584]{1,0:T(8,128)(2,1)S(1)} %get-tuple-element.106), channel_id=1, source_target_pairs={{0,4},{1,5},{2,6},{3,7},{4,0},{5,1},{6,2},{7,3},{8,12},{9,13},{10,... | collective-permute-start | bytes 172040 | tf_op jit(solution)/shard_map/ppermute | solution.py:44
  39.9 2.3 %collective-permute-done.14.refs_5_ = bf16[8,3584]{1,0:T(8,128)(2,1)S(1)} collective-permute-done((bf16[8,3584]{1,0:T(8,128)(2,1)S(1)}, bf16[8,3584]{1,0:T(8,128)(2,1)S(1)}, u32[]{:S(2)}, u32[]{:S(2)}) %collective-permute-start.14) | collective-permute-done | bytes 57376 | tf_op jit(solution)/shard_map/ppermute | solution.py:44
  42.3 2.0 %collective-permute-start.16 = (bf16[8,3584]{1,0:T(8,128)(2,1)S(1)}, bf16[8,3584]{1,0:T(8,128)(2,1)S(1)}, u32[]{:S(2)}, u32[]{:S(2)}) collective-permute-start(bf16[8,3584]{1,0:T(8,128)(2,1)S(1)} %get-tuple-element.107), channel_id=1, source_target_pairs={{0,6},{1,7},{2,4},{3,5},{4,2},{5,3},{6,0},{7,1},{8,14},{9,15},{10,... | collective-permute-start | bytes 172040 | tf_op jit(solution)/shard_map/ppermute | solution.py:44
  44.3 0.0 collective-permute-done.15.refs_6_
  44.3 3.0 %collective-permute-done.16.refs_7_ = bf16[8,3584]{1,0:T(8,128)(2,1)S(1)} collective-permute-done((bf16[8,3584]{1,0:T(8,128)(2,1)S(1)}, bf16[8,3584]{1,0:T(8,128)(2,1)S(1)}, u32[]{:S(2)}, u32[]{:S(2)}) %collective-permute-start.16) | collective-permute-done | bytes 57376 | tf_op jit(solution)/shard_map/ppermute | solution.py:44
  47.3 0.0 collective-permute-done.11.refs_1_
  47.3 0.0 collective-permute-done.12.refs_2_
  47.3 0.0 collective-permute-done.13.refs_3_
  47.4 2.6 %shard_map.128 = (bf16[8,7168]{1,0:T(8,128)(2,1)S(1)}, bf16[8,7168]{1,0:T(8,128)(2,1)S(1)}, bf16[8,7168]{1,0:T(8,128)(2,1)S(1)}, bf16[8,7168]{1,0:T(8,128)(2,1)S(1)}) custom-call(f32[1,3584]{1,0:T(1,128)S(1)} %copy-done.1, bf16[3584,512]{1,0:T(8,128)(2,1)S(1)} %get-tuple-element.78.cols_ref, bf16[256,3584]{1,0:T(8,128)(2,1)S(1)} %get-tuple-element.79.rows_ref, ...), custom_call_target="tpu_custom_call" | custom-call | tf_op jit(solution)/shard_map/pallas_call | solution.py:22
  50.0 1.5 %collective-permute-start.17 = (bf16[8,7168]{1,0:T(8,128)(2,1)S(1)}, bf16[8,7168]{1,0:T(8,128)(2,1)S(1)}, u32[]{:S(2)}, u32[]{:S(2)}) collective-permute-start(bf16[8,7168]{1,0:T(8,128)(2,1)S(1)} %get-tuple-element.109), channel_id=1, source_target_pairs={{0,2},{1,3},{2,0},{3,1},{4,6},{5,7},{6,4},{7,5},{8,10},{9,11},{10,... | collective-permute-start | bytes 344072 | tf_op jit(solution)/shard_map/ppermute | solution.py:44
  51.5 1.1 %collective-permute-start.18 = (bf16[8,7168]{1,0:T(8,128)(2,1)S(1)}, bf16[8,7168]{1,0:T(8,128)(2,1)S(1)}, u32[]{:S(2)}, u32[]{:S(2)}) collective-permute-start(bf16[8,7168]{1,0:T(8,128)(2,1)S(1)} %get-tuple-element.110), channel_id=1, source_target_pairs={{0,4},{1,5},{2,6},{3,7},{4,0},{5,1},{6,2},{7,3},{8,12},{9,13},{10,... | collective-permute-start | bytes 344072 | tf_op jit(solution)/shard_map/ppermute | solution.py:44
  52.7 0.9 %collective-permute-start.19 = (bf16[8,7168]{1,0:T(8,128)(2,1)S(1)}, bf16[8,7168]{1,0:T(8,128)(2,1)S(1)}, u32[]{:S(2)}, u32[]{:S(2)}) collective-permute-start(bf16[8,7168]{1,0:T(8,128)(2,1)S(1)} %get-tuple-element.111), channel_id=1, source_target_pairs={{0,6},{1,7},{2,4},{3,5},{4,2},{5,3},{6,0},{7,1},{8,14},{9,15},{10,... | collective-permute-start | bytes 344072 | tf_op jit(solution)/shard_map/ppermute | solution.py:44
  53.6 1.3 %collective-permute-done.17.refs_1_ = bf16[8,7168]{1,0:T(8,128)(2,1)S(1)} collective-permute-done((bf16[8,7168]{1,0:T(8,128)(2,1)S(1)}, bf16[8,7168]{1,0:T(8,128)(2,1)S(1)}, u32[]{:S(2)}, u32[]{:S(2)}) %collective-permute-start.17) | collective-permute-done | bytes 114720 | tf_op jit(solution)/shard_map/ppermute | solution.py:44
  54.9 1.5 %collective-permute-done.18.refs_2_ = bf16[8,7168]{1,0:T(8,128)(2,1)S(1)} collective-permute-done((bf16[8,7168]{1,0:T(8,128)(2,1)S(1)}, bf16[8,7168]{1,0:T(8,128)(2,1)S(1)}, u32[]{:S(2)}, u32[]{:S(2)}) %collective-permute-start.18) | collective-permute-done | bytes 114720 | tf_op jit(solution)/shard_map/ppermute | solution.py:44
  56.3 2.0 %collective-permute-done.19.refs_3_ = bf16[8,7168]{1,0:T(8,128)(2,1)S(1)} collective-permute-done((bf16[8,7168]{1,0:T(8,128)(2,1)S(1)}, bf16[8,7168]{1,0:T(8,128)(2,1)S(1)}, u32[]{:S(2)}, u32[]{:S(2)}) %collective-permute-start.19) | collective-permute-done | bytes 114720 | tf_op jit(solution)/shard_map/ppermute | solution.py:44
  58.4 0.9 %shard_map.129 = (bf16[24,3584]{1,0:T(8,128)(2,1)}, bf16[24,3584]{1,0:T(8,128)(2,1)}) custom-call(bf16[4,24,32]{2,1,0:T(8,128)(2,1)S(1)} %get-tuple-element.77.tables, bf16[8,7168]{1,0:T(8,128)(2,1)S(1)} %get-tuple-element.108.refs_0_, bf16[8,7168]{1,0:T(8,128)(2,1)S(1)} %collective-permute-done.17.refs_1_, ...), custom_call_target="tpu_custom_call" | custom-call | tf_op jit(solution)/shard_map/pallas_call | solution.py:22
Async XLA Ops:
  0.6 15.5 %copy-start.1 = (f32[1,3584]{1,0:T(1,128)S(1)}, f32[1,3584]{1,0:T(1,128)}, u32[]{:S(2)}) copy-start(f32[1,3584]{1,0:T(1,128)} %gain_ref.3) | copy-start | bytes 43012
  2.3 5.2 %collective-permute-start = (bf16[3584,128]{1,0:T(8,128)(2,1)}, bf16[3584,128]{1,0:T(8,128)(2,1)S(1)}, u32[]{:S(2)}, u32[]{:S(2)}) collective-permute-start(bf16[3584,128]{1,0:T(8,128)(2,1)} %bitcast.14), channel_id=1, source_target_pairs={{0,1},{1,0},{2,3},{3,2},{4,5},{5,4},{6,7},{7,6},{8,9},{9,8},{10,11... | collective-permute-start | bytes 2752520 | tf_op jit(solution)/shard_map/ppermute | solution.py:37
  2.8 7.4 %collective-permute-start.1 = (bf16[3584,128]{1,0:T(8,128)(2,1)}, bf16[3584,128]{1,0:T(8,128)(2,1)S(1)}, u32[]{:S(2)}, u32[]{:S(2)}) collective-permute-start(bf16[3584,128]{1,0:T(8,128)(2,1)} %bitcast.16), channel_id=1, source_target_pairs={{0,1},{1,0},{2,3},{3,2},{4,5},{5,4},{6,7},{7,6},{8,9},{9,8},{10,11... | collective-permute-start | bytes 2752520 | tf_op jit(solution)/shard_map/ppermute | solution.py:37
  2.9 7.4 %collective-permute-start.2 = (bf16[128,3584]{1,0:T(8,128)(2,1)}, bf16[128,3584]{1,0:T(8,128)(2,1)S(1)}, u32[]{:S(2)}, u32[]{:S(2)}) collective-permute-start(bf16[128,3584]{1,0:T(8,128)(2,1)} %bitcast.18), channel_id=1, source_target_pairs={{0,1},{1,0},{2,3},{3,2},{4,5},{5,4},{6,7},{7,6},{8,9},{9,8},{10,11... | collective-permute-start | bytes 2752520 | tf_op jit(solution)/shard_map/ppermute | solution.py:37
  3.4 9.6 %collective-permute-start.3 = (bf16[8,10880]{1,0:T(8,128)(2,1)S(1)}, bf16[8,10880]{1,0:T(8,128)(2,1)S(1)}, u32[]{:S(2)}, u32[]{:S(2)}) collective-permute-start(bf16[8,10880]{1,0:T(8,128)(2,1)S(1)} %get-tuple-element.85), channel_id=1, source_target_pairs={{0,2},{1,3},{2,0},{3,1},{4,6},{5,7},{6,4},{7,5},{8,10},{9,11},{10,... | collective-permute-start | bytes 522248 | tf_op jit(solution)/shard_map/ppermute | solution.py:44
  5.9 10.2 %collective-permute-start.4 = (bf16[8,10880]{1,0:T(8,128)(2,1)S(1)}, bf16[8,10880]{1,0:T(8,128)(2,1)S(1)}, u32[]{:S(2)}, u32[]{:S(2)}) collective-permute-start(bf16[8,10880]{1,0:T(8,128)(2,1)S(1)} %get-tuple-element.86), channel_id=1, source_target_pairs={{0,4},{1,5},{2,6},{3,7},{4,0},{5,1},{6,2},{7,3},{8,12},{9,13},{10,... | collective-permute-start | bytes 522248 | tf_op jit(solution)/shard_map/ppermute | solution.py:44
  7.4 8.7 %collective-permute-start.5 = (bf16[8,10880]{1,0:T(8,128)(2,1)S(1)}, bf16[8,10880]{1,0:T(8,128)(2,1)S(1)}, u32[]{:S(2)}, u32[]{:S(2)}) collective-permute-start(bf16[8,10880]{1,0:T(8,128)(2,1)S(1)} %get-tuple-element.87), channel_id=1, source_target_pairs={{0,6},{1,7},{2,4},{3,5},{4,2},{5,3},{6,0},{7,1},{8,14},{9,15},{10,... | collective-permute-start | bytes 522248 | tf_op jit(solution)/shard_map/ppermute | solution.py:44
  9.0 1.0 %copy-start = (bf16[1,2,24,3584]{3,2,1,0:T(8,128)(2,1)S(1)}, bf16[1,2,24,3584]{3,2,1,0:T(8,128)(2,1)}, u32[]{:S(2)}) copy-start(bf16[1,2,24,3584]{3,2,1,0:T(8,128)(2,1)} %param.13) | copy-start | bytes 1032196
  18.8 5.3 %collective-permute-start.6 = (bf16[8,7168]{1,0:T(8,128)(2,1)S(1)}, bf16[8,7168]{1,0:T(8,128)(2,1)S(1)}, u32[]{:S(2)}, u32[]{:S(2)}) collective-permute-start(bf16[8,7168]{1,0:T(8,128)(2,1)S(1)} %get-tuple-element.89), channel_id=1, source_target_pairs={{0,2},{1,3},{2,0},{3,1},{4,6},{5,7},{6,4},{7,5},{8,10},{9,11},{10,... | collective-permute-start | bytes 344072 | tf_op jit(solution)/shard_map/ppermute | solution.py:44
  20.1 6.9 %collective-permute-start.7 = (bf16[8,7168]{1,0:T(8,128)(2,1)S(1)}, bf16[8,7168]{1,0:T(8,128)(2,1)S(1)}, u32[]{:S(2)}, u32[]{:S(2)}) collective-permute-start(bf16[8,7168]{1,0:T(8,128)(2,1)S(1)} %get-tuple-element.90), channel_id=1, source_target_pairs={{0,4},{1,5},{2,6},{3,7},{4,0},{5,1},{6,2},{7,3},{8,12},{9,13},{10,... | collective-permute-start | bytes 344072 | tf_op jit(solution)/shard_map/ppermute | solution.py:44
  20.9 6.1 %collective-permute-start.8 = (bf16[8,7168]{1,0:T(8,128)(2,1)S(1)}, bf16[8,7168]{1,0:T(8,128)(2,1)S(1)}, u32[]{:S(2)}, u32[]{:S(2)}) collective-permute-start(bf16[8,7168]{1,0:T(8,128)(2,1)S(1)} %get-tuple-element.91), channel_id=1, source_target_pairs={{0,6},{1,7},{2,4},{3,5},{4,2},{5,3},{6,0},{7,1},{8,14},{9,15},{10,... | collective-permute-start | bytes 344072 | tf_op jit(solution)/shard_map/ppermute | solution.py:44
  27.2 5.5 %collective-permute-start.10 = (bf16[24,3584]{1,0:T(8,128)(2,1)S(1)}, bf16[24,3584]{1,0:T(8,128)(2,1)S(1)}, u32[]{:S(2)}, u32[]{:S(2)}) collective-permute-start(bf16[24,3584]{1,0:T(8,128)(2,1)S(1)} %get-tuple-element.99), channel_id=1, source_target_pairs={{0,2},{1,3},{2,0},{3,1},{4,6},{5,7},{6,4},{7,5},{8,16},{9,17},{10,... | collective-permute-start | bytes 516104 | tf_op jit(solution)/shard_map/ppermute | solution.py:55
  28.4 5.4 %collective-permute-start.9 = (bf16[24,3584]{1,0:T(8,128)(2,1)S(1)}, bf16[24,3584]{1,0:T(8,128)(2,1)S(1)}, u32[]{:S(2)}, u32[]{:S(2)}) collective-permute-start(bf16[24,3584]{1,0:T(8,128)(2,1)S(1)} %get-tuple-element.98), channel_id=1, source_target_pairs={{0,8},{1,9},{2,10},{3,11},{4,12},{5,13},{6,14},{7,15},{8,0},{9,1},... | collective-permute-start | bytes 516104 | tf_op jit(solution)/shard_map/ppermute | solution.py:55
  34.1 13.2 %collective-permute-start.11 = (bf16[8,7296]{1,0:T(8,128)(2,1)S(1)}, bf16[8,7296]{1,0:T(8,128)(2,1)S(1)}, u32[]{:S(2)}, u32[]{:S(2)}) collective-permute-start(bf16[8,7296]{1,0:T(8,128)(2,1)S(1)} %get-tuple-element.101), channel_id=1, source_target_pairs={{0,2},{1,3},{2,0},{3,1},{4,6},{5,7},{6,4},{7,5},{8,10},{9,11},{10,... | collective-permute-start | bytes 350216 | tf_op jit(solution)/shard_map/ppermute | solution.py:44
  35.3 12.0 %collective-permute-start.12 = (bf16[8,7296]{1,0:T(8,128)(2,1)S(1)}, bf16[8,7296]{1,0:T(8,128)(2,1)S(1)}, u32[]{:S(2)}, u32[]{:S(2)}) collective-permute-start(bf16[8,7296]{1,0:T(8,128)(2,1)S(1)} %get-tuple-element.102), channel_id=1, source_target_pairs={{0,4},{1,5},{2,6},{3,7},{4,0},{5,1},{6,2},{7,3},{8,12},{9,13},{10,... | collective-permute-start | bytes 350216 | tf_op jit(solution)/shard_map/ppermute | solution.py:44
  36.4 10.9 %collective-permute-start.13 = (bf16[8,7296]{1,0:T(8,128)(2,1)S(1)}, bf16[8,7296]{1,0:T(8,128)(2,1)S(1)}, u32[]{:S(2)}, u32[]{:S(2)}) collective-permute-start(bf16[8,7296]{1,0:T(8,128)(2,1)S(1)} %get-tuple-element.103), channel_id=1, source_target_pairs={{0,6},{1,7},{2,4},{3,5},{4,2},{5,3},{6,0},{7,1},{8,14},{9,15},{10,... | collective-permute-start | bytes 350216 | tf_op jit(solution)/shard_map/ppermute | solution.py:44
  37.7 4.6 %collective-permute-start.14 = (bf16[8,3584]{1,0:T(8,128)(2,1)S(1)}, bf16[8,3584]{1,0:T(8,128)(2,1)S(1)}, u32[]{:S(2)}, u32[]{:S(2)}) collective-permute-start(bf16[8,3584]{1,0:T(8,128)(2,1)S(1)} %get-tuple-element.105), channel_id=1, source_target_pairs={{0,2},{1,3},{2,0},{3,1},{4,6},{5,7},{6,4},{7,5},{8,10},{9,11},{10,... | collective-permute-start | bytes 172040 | tf_op jit(solution)/shard_map/ppermute | solution.py:44
  38.8 5.5 %collective-permute-start.15 = (bf16[8,3584]{1,0:T(8,128)(2,1)S(1)}, bf16[8,3584]{1,0:T(8,128)(2,1)S(1)}, u32[]{:S(2)}, u32[]{:S(2)}) collective-permute-start(bf16[8,3584]{1,0:T(8,128)(2,1)S(1)} %get-tuple-element.106), channel_id=1, source_target_pairs={{0,4},{1,5},{2,6},{3,7},{4,0},{5,1},{6,2},{7,3},{8,12},{9,13},{10,... | collective-permute-start | bytes 172040 | tf_op jit(solution)/shard_map/ppermute | solution.py:44
  42.3 5.1 %collective-permute-start.16 = (bf16[8,3584]{1,0:T(8,128)(2,1)S(1)}, bf16[8,3584]{1,0:T(8,128)(2,1)S(1)}, u32[]{:S(2)}, u32[]{:S(2)}) collective-permute-start(bf16[8,3584]{1,0:T(8,128)(2,1)S(1)} %get-tuple-element.107), channel_id=1, source_target_pairs={{0,6},{1,7},{2,4},{3,5},{4,2},{5,3},{6,0},{7,1},{8,14},{9,15},{10,... | collective-permute-start | bytes 172040 | tf_op jit(solution)/shard_map/ppermute | solution.py:44
  50.0 4.9 %collective-permute-start.17 = (bf16[8,7168]{1,0:T(8,128)(2,1)S(1)}, bf16[8,7168]{1,0:T(8,128)(2,1)S(1)}, u32[]{:S(2)}, u32[]{:S(2)}) collective-permute-start(bf16[8,7168]{1,0:T(8,128)(2,1)S(1)} %get-tuple-element.109), channel_id=1, source_target_pairs={{0,2},{1,3},{2,0},{3,1},{4,6},{5,7},{6,4},{7,5},{8,10},{9,11},{10,... | collective-permute-start | bytes 344072 | tf_op jit(solution)/shard_map/ppermute | solution.py:44
  51.5 4.8 %collective-permute-start.18 = (bf16[8,7168]{1,0:T(8,128)(2,1)S(1)}, bf16[8,7168]{1,0:T(8,128)(2,1)S(1)}, u32[]{:S(2)}, u32[]{:S(2)}) collective-permute-start(bf16[8,7168]{1,0:T(8,128)(2,1)S(1)} %get-tuple-element.110), channel_id=1, source_target_pairs={{0,4},{1,5},{2,6},{3,7},{4,0},{5,1},{6,2},{7,3},{8,12},{9,13},{10,... | collective-permute-start | bytes 344072 | tf_op jit(solution)/shard_map/ppermute | solution.py:44
  52.7 5.7 %collective-permute-start.19 = (bf16[8,7168]{1,0:T(8,128)(2,1)S(1)}, bf16[8,7168]{1,0:T(8,128)(2,1)S(1)}, u32[]{:S(2)}, u32[]{:S(2)}) collective-permute-start(bf16[8,7168]{1,0:T(8,128)(2,1)S(1)} %get-tuple-element.111), channel_id=1, source_target_pairs={{0,6},{1,7},{2,4},{3,5},{4,2},{5,3},{6,0},{7,1},{8,14},{9,15},{10,... | collective-permute-start | bytes 344072 | tf_op jit(solution)/shard_map/ppermute | solution.py:44
